TPU v7x, 256 devices: a whole 4x4x8 slice. The times are simulated.
256 devices in a mesh: wide: 64 (over x, z_lo, y, core), narrow: 4 (over z_hi).
Axes of the slice: x: 4, y: 4, z: 8 (z_hi: 4, z_lo: 2; z = z_hi * 2 + z_lo), core: 2. Of those that a mesh axis runs over, the one named last changes fastest.
Arguments:
- token_ids: int32 [128], P('wide'), may hold values from 0 to 65535
- attr_ids: int32 [128], replicated, may hold values from 0 to 65535
- target: int32 [128], P('wide'), may hold values from 0 to 127
- loss_mask: int32 [128], P('wide'), may hold values 0 or 1
- embed_table: bfloat16 [65536, 8192], P('wide', 'narrow'), may hold values from -30 to 30
- norm_gain: float32 [8192], P('narrow'), may hold values from 0.1 to 1.9
- w_gate: bfloat16 [8192, 28672], P('narrow', 'wide'), may hold values from -0.0625 to 0.0625
- w_up: bfloat16 [8192, 28672], P('narrow', 'wide'), may hold values from -0.0625 to 0.0625
- w_down: bfloat16 [28672, 8192], P('wide', 'narrow'), may hold values from -0.03125 to 0.03125
Outputs:
- grad_embed: bfloat16 [128, 8192], P('wide', 'narrow')
All inputs are finite; a program needn't handle non-finite values. No bound on the sum of `loss_mask` on one device may be relied on, other than what follows from the above.
Results may differ from a plain program's by a relative error of at most 0.039.
Values may be sent and summed in bfloat16 or wider, within the bound.
No kernel may reach another device: no remote copies, remote signals or barrier semaphores. Data moves between devices by JAX's collectives and lax.ppermute only.
A program may use at most 64 MiB of HBM per device.

v0:
```python
import math

import jax
import jax.numpy as jnp
from jax import lax
from jax.sharding import PartitionSpec as P

D = 8192


EPS = 1e-05


def contract_last(left_rows, right_rows):
    return lax.dot_general(
        left_rows, right_rows, (((1,), (1,)), ((), ())), preferred_element_type=jnp.float32
    )


def head_grad(logits, labels, keep_mask, probe_b):
    probability = jax.nn.softmax(logits, axis=1)
    onehot = (labels[:, None] == jnp.arange(probability.shape[1], dtype=jnp.int32)[None, :]).astype(
        jnp.float32
    )
    logit_grad = ((probability - onehot) * keep_mask[:, None].astype(jnp.float32)).astype(
        jnp.bfloat16
    )
    return jnp.dot(logit_grad, probe_b, preferred_element_type=jnp.float32)


def body(token_ids, attr_ids, target, loss_mask, embed_table, norm_gain, w_gate, w_up, w_down):
    my_index = lax.axis_index("wide")
    tok_dev = token_ids.shape[0]
    vocab_rows = embed_table.shape[0]
    low_row = my_index * vocab_rows
    logit_scale = 3.0 / math.sqrt(D)

    def lookup(wanted_ids):
        local_ids = wanted_ids - low_row
        inside = (local_ids >= 0) & (local_ids < vocab_rows)
        picked = jnp.take(embed_table, jnp.clip(local_ids, 0, vocab_rows - 1), axis=0)
        return jnp.where(inside[:, None], picked, jnp.zeros_like(picked))

    all_ids = lax.all_gather(token_ids, "wide", axis=0, tiled=True)
    rows_own = lax.psum_scatter(
        lookup(all_ids).astype(jnp.float32), "wide", scatter_dimension=0, tiled=True
    )
    probe_full = lax.psum(lookup(attr_ids).astype(jnp.float32), "wide")
    all_target, all_mask = (
        lax.all_gather(target, "wide", axis=0, tiled=True),
        lax.all_gather(loss_mask, "wide", axis=0, tiled=True),
    )
    rows_all = lax.all_gather(rows_own.astype(jnp.bfloat16), "wide", axis=0, tiled=True).astype(
        jnp.float32
    )
    squares = lax.psum(jnp.sum(rows_all * rows_all, axis=1), "narrow")
    inv_all = lax.rsqrt(squares / D + EPS)[:, None]
    normed = (rows_all * inv_all * norm_gain).astype(jnp.bfloat16)
    gate_part = jnp.dot(normed, w_gate, preferred_element_type=jnp.float32)
    up_part = jnp.dot(normed, w_up, preferred_element_type=jnp.float32)
    pair_part = jnp.concatenate([gate_part, up_part], axis=1)
    inv_own = lax.dynamic_slice_in_dim(inv_all, my_index * tok_dev, tok_dev, 0)
    probe_b = probe_full.astype(jnp.bfloat16)
    gate_up = lax.psum(pair_part, "narrow")
    ff_width = w_gate.shape[1]
    gate_pre = gate_up[:, :ff_width]
    up_pre = gate_up[:, ff_width:]
    gate_sigmoid = jax.nn.sigmoid(gate_pre)
    hidden = (gate_pre * gate_sigmoid * up_pre).astype(jnp.bfloat16)
    block_all = rows_all + lax.psum(
        jnp.dot(hidden, w_down, preferred_element_type=jnp.float32), "wide"
    )
    logits = (
        lax.psum(contract_last(block_all.astype(jnp.bfloat16), probe_b), "narrow") * logit_scale
    )
    grad_all = head_grad(logits, all_target, all_mask, probe_b)
    hidden_part = contract_last(grad_all.astype(jnp.bfloat16), w_down)
    out_grad = lax.dynamic_slice_in_dim(grad_all, my_index * tok_dev, tok_dev, 0)
    hidden_grad = lax.psum(hidden_part, "narrow")
    gate_grad = (
        hidden_grad * up_pre * gate_sigmoid * (1.0 + gate_pre * (1.0 - gate_sigmoid))
    ).astype(jnp.bfloat16)
    up_grad = (hidden_grad * gate_pre * gate_sigmoid).astype(jnp.bfloat16)
    normed_grad = lax.psum_scatter(
        contract_last(gate_grad, w_gate) + contract_last(up_grad, w_up),
        "wide",
        scatter_dimension=0,
        tiled=True,
    )
    scaled = normed_grad * norm_gain
    inner = lax.psum(jnp.sum(scaled * rows_own, axis=1), "narrow")[:, None] / D
    result = out_grad + inv_own * (scaled - rows_own * inv_own * inv_own * inner)
    return result.astype(jnp.bfloat16)


def solution(mesh):
    return jax.shard_map(
        body,
        mesh=mesh,
        in_specs=(
            P("wide"),
            P(),
            P("wide"),
            P("wide"),
            P("wide", "narrow"),
            P("narrow"),
            P("narrow", "wide"),
            P("narrow", "wide"),
            P("wide", "narrow"),
        ),
        out_specs=P("wide", "narrow"),
        check_vma=False,
    )
```

profile of v0, /device:TPU:1, one launch (start us, length us, event | category | flops | bytes accessed | tf_op | source)
XLA Modules:
  0.0 1965.8 jit_solution(3734469777858977049)
XLA Ops:
  6.5 1.5 fusion.25
  11.3 17.1 all-reduce.5
  29.1 4.2 gather_fusion
  33.3 1.2 fusion.2
  34.6 5.0 gather_fusion.1
  40.2 547.1 %all-reduce.22.cloned.1.call-done = f32[128,2048]{1,0:T(8,128)} async-done(((f32[128,2048]{1,0:T(8,128)}), f32[128,2048]{1,0:T(8,128)}) %all-reduce.22.cloned.1.call-update) | async-done | bytes 1048592
  588.2 83.0 %all-gather = bf16[64,2,2048]{2,1,0:T(2,128)(2,1)S(1)} all-gather(bf16[1,2,2048]{2,1,0:T(2,128)(2,1)S(1)} %convert_bitcast_fusion), channel_id=1, replica_groups=mesh['wide'=64,'narrow'=4] {'wide'}, dimensions={0}, use_global_device_ids=true | all-gather | bytes 532480 | tf_op jit(solution)/shard_map/all_gather | solution.py:53
  671.4 9.8 psum.49
  681.3 2.3 fusion.24
  685.3 1.2 fusion.1
  686.4 45.0 %all-reduce.14.cloned.1.call-done = f32[128,896]{0,1:T(8,128)} async-done(((f32[128,896]{0,1:T(8,128)}), f32[128,896]{0,1:T(8,128)}) %all-reduce.14.cloned.1.call-update) | async-done | bytes 458768 | tf_op jit(solution)/shard_map/psum | solution.py:64
  731.4 2.5 fusion.8
  734.0 284.5 %all-reduce.25 = bf16[128,2048]{1,0:T(8,128)(2,1)S(1)} all-reduce(f32[128,2048]{1,0:T(8,128)} %fusion.1), channel_id=1, replica_groups=mesh['wide'=64,'narrow'=4] {'wide'}, use_global_device_ids=true, to_apply=%region_5.7 | all-reduce | flops 262144 | bytes 1572864 | tf_op jit(solution)/shard_map/psum | solution.py:48
  1018.5 268.0 %all-reduce.16.cloned.1.call-done = f32[128,2048]{1,0:T(8,128)} async-done(((f32[128,2048]{1,0:T(8,128)}), f32[128,2048]{1,0:T(8,128)}) %all-reduce.16.cloned.1.call-update) | async-done | bytes 1048592 | tf_op jit(solution)/shard_map/psum | solution.py:70
  1286.6 2.2 fusion
  1288.8 47.7 %all-reduce.18.cloned.1.call-done = f32[128,128]{1,0:T(8,128)} async-done(((f32[128,128]{1,0:T(8,128)}), f32[128,128]{1,0:T(8,128)}) %all-reduce.18.cloned.1.call-update) | async-done | bytes 65552 | tf_op jit(solution)/shard_map/psum | solution.py:74
  1338.5 1.2 fusion.5
  1339.7 1.3 fusion.3
  1341.1 49.6 %all-reduce.20.cloned.1.call-done = f32[128,448]{0,1:T(8,128)} async-done(((f32[128,448]{0,1:T(8,128)}), f32[128,448]{0,1:T(8,128)}) %all-reduce.20.cloned.1.call-update) | async-done | bytes 229392 | tf_op jit(solution)/shard_map/psum | solution.py:79
  1390.7 2.3 fusion.9
  1393.0 1.5 convolution_add_fusion
  1394.5 551.9 %all-reduce.24.cloned.1.call-done = f32[128,2048]{1,0:T(8,128)} async-done(((f32[128,2048]{1,0:T(8,128)}), f32[128,2048]{1,0:T(8,128)}) %all-reduce.24.cloned.1.call-update) | async-done | bytes 1048592
  1947.6 9.8 psum.55
  1957.4 1.6 add_convert_fusion.2
  (47 shorter events, 9.3 us)
Async XLA Ops:
  6.5 724.9 %copy-start = (bf16[448,2048]{1,0:T(8,128)(2,1)S(1)}, bf16[448,2048]{1,0:T(8,128)(2,1)}, u32[]{:S(2)}) copy-start(bf16[448,2048]{1,0:T(8,128)(2,1)} %param.19) | copy-start | bytes 5505028
  6.5 580.8 %all-reduce.22.cloned.1.call-start = ((), (), s32[]{:S(2)}) async-start(), calls=%async_computation.4 | async-start | bytes 2097152
  34.5 696.9 %all-reduce.14.cloned.1.call-start = ((), (), s32[]{:S(2)}) async-start(), calls=%async_computation | async-start | bytes 917504 | tf_op jit(solution)/shard_map/psum | solution.py:64
  39.5 641.8 %copy-start.6 = (f32[2048]{0:T(1024)S(1)}, f32[2048]{0:T(1024)}, u32[]{:S(2)}) copy-start(f32[2048]{0:T(1024)} %param.16) | copy-start | bytes 24580
  681.3 2.4 copy-start.1
  683.6 1.6 copy-start.3
  685.2 601.4 %all-reduce.16.cloned.1.call-start = ((), (), s32[]{:S(2)}) async-start(), calls=%async_computation.1 | async-start | bytes 2097152 | tf_op jit(solution)/shard_map/psum | solution.py:70
  734.0 602.5 %all-reduce.18.cloned.1.call-start = ((), (), s32[]{:S(2)}) async-start(), calls=%async_computation.2 | async-start | bytes 131072 | tf_op jit(solution)/shard_map/psum | solution.py:74
  1288.8 101.9 %all-reduce.20.cloned.1.call-start = ((), (), s32[]{:S(2)}) async-start(), calls=%async_computation.3 | async-start | bytes 458752 | tf_op jit(solution)/shard_map/psum | solution.py:79
  1339.7 51.0 %copy-start.4 = (f32[128,896]{0,1:T(8,128)S(1)}, f32[128,896]{0,1:T(8,128)}, u32[]{:S(2)}) copy-start(f32[128,896]{0,1:T(8,128)} %all-reduce.14.cloned.1.call-done) | copy-start | bytes 1376260
  1341.1 605.4 %all-reduce.24.cloned.1.call-start = ((), (), s32[]{:S(2)}) async-start(), calls=%async_computation.5 | async-start | bytes 2097152
  1390.7 2.3 copy-start.2
  1390.7 2.3 copy-start.5
Sparse Core Ops, SparseCore 0:
  34.6 552.6 all-reduce.21
  685.3 46.0 all-reduce.13
  734.1 552.4 all-reduce.15
  1289.2 47.2 all-reduce.17
  1341.2 49.4 all-reduce.19
  1394.7 551.7 all-reduce.23
where the time goes:
time: 1970 us
  waiting for transfers between devices  1510 us (77%)
  blocking collectives  404 us (21%)
    unnamed x8, waiting for transfers between devices  1100 us
    psum x1, blocking collectives, body(): probe_full = lax.psum(lookup(attr_ids).astype(jnp.float32), 'wide')  284 us
    psum x1, waiting for transfers between devices, body(): lax.psum(jnp.dot(hidden, w_down, preferred_element_type=jnp.float32), 'wi...  268 us
    all_gather x1, blocking collectives, body(): lax.all_gather(rows_own.astype(jnp.bfloat16), 'wide', axis=0, tiled=True)  83 us
    psum x1, waiting for transfers between devices, body(): hidden_grad = lax.psum(hidden_part, 'narrow')  49.6 us
    psum x1, waiting for transfers between devices, body(): lax.psum(contract_last(block_all.astype(jnp.bfloat16), probe_b), 'narrow')  47.7 us
    psum x1, waiting for transfers between devices, body(): gate_up = lax.psum(pair_part, 'narrow')  45 us
  transfers between devices with their start and end apart: 6, of which 6 were waited for; matrix products, arithmetic and copies ran while one was open for 0% of the time, Pallas kernels for 0%

commit v1 on v0

v1 whole, which is shorter than its diff:
```python
import math

import jax
import jax.numpy as jnp
from jax import lax
from jax.sharding import PartitionSpec as P

D = 8192
EPS = 1e-05
BF = jnp.bfloat16
F32 = jnp.float32
WIRE = BF


def contract_last(left, right):
    return lax.dot_general(left, right, (((1,), (1,)), ((), ())), preferred_element_type=F32)


def split_hi_lo(value):
    high = lax.reduce_precision(value, exponent_bits=8, mantissa_bits=7)
    return high.astype(BF), (value - high).astype(BF)


def swap(blocks):
    return lax.all_to_all(blocks, "wide", 0, 0, tiled=True)


def body(token_ids, attr_ids, target, loss_mask, embed_table, norm_gain, w_gate, w_up, w_down):
    wide = lax.axis_size("wide")
    narrow = lax.axis_size("narrow")
    my_wide = lax.axis_index("wide")
    my_narrow = lax.axis_index("narrow")
    tok_dev = token_ids.shape[0]
    tokens = tok_dev * wide
    attrs = attr_ids.shape[0]
    vocab_rows, cols = embed_table.shape
    ff = w_gate.shape[1]
    logit_scale = 3.0 / math.sqrt(D)

    def shift(step):
        return [(i, (i + step) % narrow) for i in range(narrow)]

    def rows_here(ids):
        local = jnp.clip(ids - my_wide * vocab_rows, 0, vocab_rows - 1)
        return jnp.take(embed_table, local, axis=0)

    def pick(received, ids):
        owner = ids // vocab_rows
        return jnp.concatenate(
            [
                lax.dynamic_slice(received, (owner[i], i, 0), (1, 1, cols)).reshape(1, cols)
                for i in range(tok_dev)
            ],
            axis=0,
        )

    ids_high = (token_ids // 256).astype(BF)
    ids_low = (token_ids % 256).astype(BF)
    extra = jnp.stack([ids_high, ids_low], axis=1)
    extra = jnp.pad(extra, ((0, 0), (0, 126)))
    probe_out = rows_here(attr_ids).reshape(wide, tok_dev, cols)
    first = jnp.concatenate(
        [probe_out, jnp.broadcast_to(extra[None], (wide, tok_dev, 128))], axis=2
    )
    first = swap(first)
    digits = first[:, :, cols : cols + 2].astype(F32)
    all_ids = (digits[:, :, 0] * 256.0 + digits[:, :, 1]).astype(jnp.int32).reshape(tokens)
    my_attrs = lax.dynamic_slice_in_dim(attr_ids, my_wide * tok_dev, tok_dev, 0)
    probe_own = pick(first, my_attrs)

    rows_out = rows_here(all_ids).reshape(wide, tok_dev, cols)
    second = swap(
        jnp.concatenate(
            [rows_out, jnp.broadcast_to(probe_own[None], (wide, tok_dev, cols))], axis=1
        )
    )
    probe = second[:, tok_dev:, :].reshape(attrs, cols)
    rows_own = pick(second, token_ids)
    rows = swap(jnp.broadcast_to(rows_own[None], (wide, tok_dev, cols))).reshape(tokens, cols)

    down_part = contract_last(w_down, probe).astype(WIRE)
    down_sum = down_part.astype(F32)
    for step in range(1, narrow):
        down_sum = down_sum + lax.ppermute(down_part, "narrow", shift(step)).astype(F32)
    down_high, down_low = split_hi_lo(down_sum)
    down_pair = jnp.concatenate([down_high, down_low], axis=1)

    own_high, own_low = split_hi_lo(contract_last(probe, rows_own))
    rows_f = rows.astype(F32)
    scaled_rows = (rows_f * norm_gain).astype(BF)
    gate_part = jnp.dot(scaled_rows, w_gate, preferred_element_type=F32)
    up_part = jnp.dot(scaled_rows, w_up, preferred_element_type=F32)
    sq_high, sq_low = split_hi_lo(jnp.sum(rows_f * rows_f, axis=1, keepdims=True))
    part = jnp.concatenate(
        [
            gate_part.astype(BF),
            up_part.astype(BF),
            sq_high,
            sq_low,
            own_high,
            own_low,
            jnp.zeros((tokens, 122), BF),
        ],
        axis=1,
    )
    summed = part.astype(F32)
    for step in range(1, narrow):
        summed = summed + lax.ppermute(part, "narrow", shift(step)).astype(F32)
    squares = summed[:, 2 * ff : 2 * ff + 1] + summed[:, 2 * ff + 1 : 2 * ff + 2]
    inv_all = lax.rsqrt(squares / D + EPS)
    gate_pre = summed[:, :ff] * inv_all
    up_pre = summed[:, ff : 2 * ff] * inv_all
    own_logits = (
        summed[:, 2 * ff + 2 : 2 * ff + 4] + summed[:, 2 * ff + 4 : 2 * ff + 6]
    ).T
    inv_own = lax.dynamic_slice_in_dim(inv_all, my_wide * tok_dev, tok_dev, 0)

    gate_sigmoid = jax.nn.sigmoid(gate_pre)
    hidden = (gate_pre * gate_sigmoid * up_pre).astype(BF)
    logit_pair = jnp.dot(hidden, down_pair, preferred_element_type=F32)
    logit_part = logit_pair[:, :attrs] + logit_pair[:, attrs:]
    logit_sum = jnp.sum(swap(logit_part.reshape(wide, tok_dev, attrs)), axis=0)
    logits = (logit_sum + own_logits) * logit_scale
    probability = jax.nn.softmax(logits, axis=1)
    onehot = (target[:, None] == jnp.arange(attrs, dtype=jnp.int32)[None, :]).astype(F32)
    grad_own = ((probability - onehot) * loss_mask[:, None].astype(F32)).astype(BF)
    logit_grad = swap(jnp.broadcast_to(grad_own[None], (wide, tok_dev, attrs))).reshape(
        tokens, attrs
    )
    out_grad = jnp.dot(grad_own, probe, preferred_element_type=F32)

    hidden_grad = contract_last(logit_grad, down_high)
    gate_grad = (
        hidden_grad * up_pre * gate_sigmoid * (1.0 + gate_pre * (1.0 - gate_sigmoid))
    ).astype(BF)
    up_grad = (hidden_grad * gate_pre * gate_sigmoid).astype(BF)
    inner_part = jnp.sum(
        gate_grad.astype(F32) * gate_pre + up_grad.astype(F32) * up_pre, axis=1, keepdims=True
    )
    inner_high, inner_low = split_hi_lo(inner_part)
    normed_part = contract_last(gate_grad, w_gate) + contract_last(up_grad, w_up)
    last = jnp.concatenate(
        [normed_part.astype(BF), inner_high, inner_low, jnp.zeros((tokens, 126), BF)], axis=1
    )
    last = swap(last.reshape(wide, tok_dev, cols + 128))
    last = jnp.sum(last.astype(F32), axis=0)
    scaled = last[:, :cols] * norm_gain
    inner = last[:, cols : cols + 1] + last[:, cols + 1 : cols + 2]
    result = out_grad + inv_own * scaled - rows_own.astype(F32) * (inv_own * inv_own * inner / D)
    return result.astype(BF)


def solution(mesh):
    return jax.shard_map(
        body,
        mesh=mesh,
        in_specs=(
            P("wide"),
            P(),
            P("wide"),
            P("wide"),
            P("wide", "narrow"),
            P("narrow"),
            P("narrow", "wide"),
            P("narrow", "wide"),
            P("wide", "narrow"),
        ),
        out_specs=P("wide", "narrow"),
        check_vma=False,
    )
```

time: 1970 us -> 175 us (0.09)
  waiting for transfers between devices: 1510 us -> 60.1 us
  blocking collectives: 404 us -> 11.9 us
  starting transfers between devices: 0.21 us -> 52.5 us
    unnamed x8 -> x0, waiting for transfers between devices: 1100 us -> none
    psum x4 -> x0, waiting for transfers between devices: 410 us -> none  [the longest x1 268 us: body(): lax.psum(jnp.dot(hidden, w_down, preferred_element_type=jnp.float32), 'wi...]
    psum x3 -> x0, blocking collectives: 304 us -> none  [the longest x1 284 us: body(): probe_full = lax.psum(lookup(attr_ids).astype(jnp.float32), 'wide')]
    all_gather x1 -> x0, blocking collectives: 83 us -> none  [body(): lax.all_gather(rows_own.astype(jnp.bfloat16), 'wide', axis=0, tiled=True)]
    all_to_all x0 -> x5, waiting for transfers between devices: none -> 42.4 us  [swap(): return lax.all_to_all(blocks, 'wide', 0, 0, tiled=True)]
    all_to_all x0 -> x5, starting transfers between devices: none -> 34.7 us  [swap(): return lax.all_to_all(blocks, 'wide', 0, 0, tiled=True)]
  transfers between devices with their start and end apart: 6 -> 11, of which waited for: 6 -> 6; matrix products, arithmetic and copies ran while one was open for 0% -> 9% of each run, Pallas kernels for 0% -> 0%
where the time goes in v1:
time: 175 us; the launch traced here: 174 us
  waiting for transfers between devices  60.1 us (34%)
  starting transfers between devices  52.5 us (30%)
  local copies, waits for them, and re-layouts  22.9 us (13%)
  blocking collectives  11.9 us (7%)
  matrix products  9.66 us (6%)
  other arithmetic  9.54 us (5%)
  between operations  7.72 us (4%)
    all_to_all x5, waiting for transfers between devices, swap(): return lax.all_to_all(blocks, 'wide', 0, 0, tiled=True)  42.4 us
    all_to_all x5, starting transfers between devices, swap(): return lax.all_to_all(blocks, 'wide', 0, 0, tiled=True)  34.7 us
    ppermute x3, waiting for transfers between devices, body(): summed = summed + lax.ppermute(part, 'narrow', shift(step)).astype(F32)  17.7 us
    all_to_all x1, blocking collectives, swap(): return lax.all_to_all(blocks, 'wide', 0, 0, tiled=True)  11.9 us
    ppermute x3, starting transfers between devices, body(): summed = summed + lax.ppermute(part, 'narrow', shift(step)).astype(F32)  9.43 us
    ppermute x3, starting transfers between devices, body(): lax.ppermute(down_part, 'narrow', shift(step)).astype(F32)  8.45 us
    gather x2, local copies, waits for them, and re-layouts, rows_here(): return jnp.take(embed_table, local, axis=0)  8.34 us
    dot_general x5, matrix products, contract_last(): lax.dot_general(left, right, (((1,), (1,)), ((), ())), preferred_element_...  4.49 us
  transfers between devices with their start and end apart: 11, of which 6 were waited for; matrix products, arithmetic and copies ran while one was open for 9% of the time, Pallas kernels for 0%

profile of v1, /device:TPU:1, one launch (start us, length us, event | category | flops | bytes accessed | tf_op | source)
XLA Modules:
  0.0 174.4 jit_solution(10009356956469310002)
XLA Ops:
  1.7 4.2 %gather_fusion = bf16[128,2048]{1,0:T(8,128)(2,1)S(1)} fusion(bf16[1024,2048]{1,0:T(8,128)(2,1)} %param.15, s32[1024]{0:T(1024)S(1)} %pad_clamp_fusion.1), kind=kCustom, calls=%fused_computation.clone | custom fusion | bytes 1049088 | tf_op jit(solution)/shard_map/jit(_take)/gather | solution.py:45
  7.7 10.3 %all-to-all-start = ((bf16[64,2,2176]{2,1,0:T(2,128)(2,1)}), bf16[64,2,2176]{2,1,0:T(2,128)(2,1)S(1)}, u32[]{:S(2)}, u32[]{:S(2)}) async-start(bf16[64,2,2176]{2,1,0:T(2,128)(2,1)} %pad_maximum_fusion.1), calls=%async_computation | async-start | bytes 1114112 | tf_op jit(solution)/shard_map/all_to_all | solution.py:25
  22.4 8.4 %all-to-all-done = bf16[64,2,2176]{2,1,0:T(2,128)(2,1)S(1)} async-done(((bf16[64,2,2176]{2,1,0:T(2,128)(2,1)}), bf16[64,2,2176]{2,1,0:T(2,128)(2,1)S(1)}, u32[]{:S(2)}, u32[]{:S(2)}) %all-to-all-start) | async-done | bytes 557088 | tf_op jit(solution)/shard_map/all_to_all | solution.py:25
  31.2 4.2 %gather_fusion.1 = bf16[128,2048]{1,0:T(8,128)(2,1)S(1)} fusion(bf16[1024,2048]{1,0:T(8,128)(2,1)} %param.15, s32[1024]{0:T(1024)S(1)} %pad_clamp_fusion), kind=kCustom, calls=%fused_computation.1.clone | custom fusion | bytes 1049088 | tf_op jit(solution)/shard_map/jit(_take)/gather | solution.py:45
  36.2 2.1 %pad_maximum_fusion = bf16[64,4,2048]{2,1,0:T(4,128)(2,1)} fusion(bf16[64,2,2048]{2,1,0:T(2,128)(2,1)S(1)} %broadcast_in_dim.22, bf16[64,2,2048]{2,1,0:T(2,128)(2,1)S(1)} %reshape.131), kind=kLoop, calls=%fused_computation.12 | loop fusion | flops 2097152 | bytes 2097152 | tf_op jit(solution)/shard_map/concatenate | solution.py:73
  38.3 4.7 %all-to-all-start.1 = ((bf16[64,4,2048]{2,1,0:T(4,128)(2,1)}), bf16[64,4,2048]{2,1,0:T(4,128)(2,1)S(1)}, u32[]{:S(2)}, u32[]{:S(2)}) async-start(bf16[64,4,2048]{2,1,0:T(4,128)(2,1)} %pad_maximum_fusion), calls=%async_computation.1 | async-start | bytes 2097152 | tf_op jit(solution)/shard_map/all_to_all | solution.py:25
  47.1 13.8 %all-to-all-done.1 = bf16[64,4,2048]{2,1,0:T(4,128)(2,1)S(1)} async-done(((bf16[64,4,2048]{2,1,0:T(4,128)(2,1)}), bf16[64,4,2048]{2,1,0:T(4,128)(2,1)S(1)}, u32[]{:S(2)}, u32[]{:S(2)}) %all-to-all-start.1) | async-done | bytes 1048608 | tf_op jit(solution)/shard_map/all_to_all | solution.py:25
  62.1 4.7 %all-to-all-start.2 = ((bf16[64,2,2048]{2,1,0:T(2,128)(2,1)}), bf16[64,2,2048]{2,1,0:T(2,128)(2,1)S(1)}, u32[]{:S(2)}, u32[]{:S(2)}) async-start(bf16[64,2,2048]{2,1,0:T(2,128)(2,1)} %broadcast_in_dim.23), calls=%async_computation.2 | async-start | bytes 1048576 | tf_op jit(solution)/shard_map/all_to_all | solution.py:25
  66.8 1.8 %slice.83 = bf16[64,2,2048]{2,1,0:T(2,128)(2,1)S(1)} slice(bf16[64,4,2048]{2,1,0:T(4,128)(2,1)} %copy-done.3), slice={[0:64], [2:4], [0:2048]} | slice | bytes 1048576 | tf_op jit(solution)/shard_map/slice | solution.py:77
  68.8 2.1 %fusion.3 = bf16[448,128]{1,0:T(8,128)(2,1)S(1)} fusion(bf16[128,2048]{1,0:T(8,128)(2,1)S(1)} %reshape.136, bf16[448,2048]{1,0:T(8,128)(2,1)} %param.19), kind=kOutput, calls=%fused_computation.10 | convolution fusion | flops 234938368 | bytes 2473984 | tf_op jit(solution)/shard_map/dot_general | solution.py:16
  71.0 5.2 %collective-permute-start.5 = (bf16[448,128]{1,0:T(8,128)(2,1)S(1)}, bf16[448,128]{1,0:T(8,128)(2,1)}, u32[]{:S(2)}, u32[]{:S(2)}) collective-permute-start(bf16[448,128]{1,0:T(8,128)(2,1)S(1)} %fusion.3), channel_id=1, source_target_pairs={{0,3},{1,0},{2,1},{3,2},{4,7},{5,4},{6,5},{7,6},{8,11},{9,8},{10,9... | collective-permute-start | bytes 344072 | tf_op jit(solution)/shard_map/ppermute | solution.py:84
  77.3 2.1 %collective-permute-start.3 = (bf16[448,128]{1,0:T(8,128)(2,1)S(1)}, bf16[448,128]{1,0:T(8,128)(2,1)}, u32[]{:S(2)}, u32[]{:S(2)}) collective-permute-start(bf16[448,128]{1,0:T(8,128)(2,1)S(1)} %fusion.3), channel_id=1, source_target_pairs={{0,1},{1,2},{2,3},{3,0},{4,5},{5,6},{6,7},{7,4},{8,9},{9,10},{10,1... | collective-permute-start | bytes 344072 | tf_op jit(solution)/shard_map/ppermute | solution.py:84
  81.8 2.8 %convolution_convert_fusion.1 = bf16[128,448]{0,1:T(8,128)(2,1)} fusion(bf16[2048,448]{0,1:T(8,128)(2,1)} %param.18, f32[128,2048]{1,0:T(8,128)S(1)} %reshape.142, f32[2048]{0:T(1024)S(1)} %copy-done.6), kind=kOutput, calls=%fused_computation.8 | convolution fusion | flops 235462656 | bytes 3006464 | tf_op jit(solution)/shard_map/dot_general | solution.py:92
  85.9 2.1 %concatenate.28 = bf16[128,1024]{0,1:T(8,128)(2,1)S(1)} concatenate(bf16[128,448]{0,1:T(8,128)(2,1)} %convolution_convert_fusion.2, bf16[128,448]{0,1:T(8,128)(2,1)} %convolution_convert_fusion.1, bf16[128,1]{0,1:T(2,128)(2,1)S(1)} %get-tuple-element.28, bf16[128,1]{0,1:T(2,128)(2,1)S(1)} %get-tuple-element.27, bf16[128,2]{0,1:T(2,128)(2,1)S(1)} %get-tuple-element.24, ...), dimensions={1} | concatenate | bytes 524288 | tf_op jit(solution)/shard_map/concatenate | solution.py:94
  88.1 4.8 %collective-permute-start.2 = (bf16[128,1024]{0,1:T(8,128)(2,1)S(1)}, bf16[128,1024]{0,1:T(8,128)(2,1)S(1)}, u32[]{:S(2)}, u32[]{:S(2)}) collective-permute-start(bf16[128,1024]{0,1:T(8,128)(2,1)S(1)} %concatenate.28), channel_id=1, source_target_pairs={{0,3},{1,0},{2,1},{3,2},{4,7},{5,4},{6,5},{7,6},{8,11},{9,8},{10,9... | collective-permute-start | bytes 786440 | tf_op jit(solution)/shard_map/ppermute | solution.py:108
  92.8 2.4 %collective-permute-start.1 = (bf16[128,1024]{0,1:T(8,128)(2,1)S(1)}, bf16[128,1024]{0,1:T(8,128)(2,1)S(1)}, u32[]{:S(2)}, u32[]{:S(2)}) collective-permute-start(bf16[128,1024]{0,1:T(8,128)(2,1)S(1)} %concatenate.28), channel_id=1, source_target_pairs={{0,2},{1,3},{2,0},{3,1},{4,6},{5,7},{6,4},{7,5},{8,10},{9,11},{10,... | collective-permute-start | bytes 786440 | tf_op jit(solution)/shard_map/ppermute | solution.py:108
  95.3 2.3 %collective-permute-start = (bf16[128,1024]{0,1:T(8,128)(2,1)S(1)}, bf16[128,1024]{0,1:T(8,128)(2,1)S(1)}, u32[]{:S(2)}, u32[]{:S(2)}) collective-permute-start(bf16[128,1024]{0,1:T(8,128)(2,1)S(1)} %concatenate.28), channel_id=1, source_target_pairs={{0,1},{1,2},{2,3},{3,0},{4,5},{5,6},{6,7},{7,4},{8,9},{9,10},{10,1... | collective-permute-start | bytes 786440 | tf_op jit(solution)/shard_map/ppermute | solution.py:108
  98.7 16.7 %collective-permute-done.2 = bf16[128,1024]{0,1:T(8,128)(2,1)S(1)} collective-permute-done((bf16[128,1024]{0,1:T(8,128)(2,1)S(1)}, bf16[128,1024]{0,1:T(8,128)(2,1)S(1)}, u32[]{:S(2)}, u32[]{:S(2)}) %collective-permute-start.2) | collective-permute-done | bytes 262176 | tf_op jit(solution)/shard_map/ppermute | solution.py:108
  117.4 10.3 %all-to-all-start.3 = ((f32[64,2,128]{2,1,0:T(2,128)}), f32[64,2,128]{2,1,0:T(2,128)S(1)}, u32[]{:S(2)}, u32[]{:S(2)}) async-start(f32[64,2,128]{2,1,0:T(2,128)} %bitcast.12), calls=%async_computation.3 | async-start | bytes 131072 | tf_op jit(solution)/shard_map/all_to_all | solution.py:25
  127.7 8.1 %all-to-all-done.3 = f32[64,2,128]{2,1,0:T(2,128)S(1)} async-done(((f32[64,2,128]{2,1,0:T(2,128)}), f32[64,2,128]{2,1,0:T(2,128)S(1)}, u32[]{:S(2)}, u32[]{:S(2)}) %all-to-all-start.3) | async-done | bytes 65568 | tf_op jit(solution)/shard_map/all_to_all | solution.py:25
  136.3 11.9 %all_to_all.30 = bf16[64,2,128]{2,1,0:T(2,128)(2,1)S(1)} all-to-all(bf16[64,2,128]{2,1,0:T(2,128)(2,1)S(1)} %broadcast_in_dim.25), channel_id=1, replica_groups=mesh['wide'=64,'narrow'=4] {'wide'}, dimensions={0} | all-to-all | bytes 65536 | tf_op jit(solution)/shard_map/all_to_all | solution.py:25
  152.2 3.0 %concatenate.31 = bf16[64,2,2176]{2,1,0:T(2,128)(2,1)} concatenate(bf16[64,2,2048]{2,1,0:T(2,128)(2,1)S(1)} %concatenate.30, bf16[64,2,1]{2,1,0:T(2,128)(2,1)S(1)} %copy.68, bf16[64,2,1]{2,1,0:T(2,128)(2,1)S(1)} %copy.69, bf16[64,2,126]{2,1,0:T(2,128)(2,1)S(1)} %broadcast_in_dim.26), dimensions={2} | concatenate | bytes 1114112 | tf_op jit(solution)/shard_map/concatenate | solution.py:142
  155.2 4.7 %all-to-all-start.5 = ((bf16[64,2,2176]{2,1,0:T(2,128)(2,1)}), bf16[64,2,2176]{2,1,0:T(2,128)(2,1)S(1)}, u32[]{:S(2)}, u32[]{:S(2)}) async-start(bf16[64,2,2176]{2,1,0:T(2,128)(2,1)} %concatenate.31), calls=%async_computation.5 | async-start | bytes 1114112 | tf_op jit(solution)/shard_map/all_to_all | solution.py:25
  160.7 12.1 %all-to-all-done.5 = bf16[64,2,2176]{2,1,0:T(2,128)(2,1)S(1)} async-done(((bf16[64,2,2176]{2,1,0:T(2,128)(2,1)}), bf16[64,2,2176]{2,1,0:T(2,128)(2,1)S(1)}, u32[]{:S(2)}, u32[]{:S(2)}) %all-to-all-start.5) | async-done | bytes 557088 | tf_op jit(solution)/shard_map/all_to_all | solution.py:25
  (90 shorter events, 22.0 us)
Async XLA Ops:
  0.0 84.6 %copy-start = (bf16[2048,448]{0,1:T(8,128)(2,1)S(1)}, bf16[2048,448]{0,1:T(8,128)(2,1)}, u32[]{:S(2)}) copy-start(bf16[2048,448]{0,1:T(8,128)(2,1)} %param.17) | copy-start | bytes 5505028
  7.7 23.1 %all-to-all-start = ((bf16[64,2,2176]{2,1,0:T(2,128)(2,1)}), bf16[64,2,2176]{2,1,0:T(2,128)(2,1)S(1)}, u32[]{:S(2)}, u32[]{:S(2)}) async-start(bf16[64,2,2176]{2,1,0:T(2,128)(2,1)} %pad_maximum_fusion.1), calls=%async_computation | async-start | bytes 1114112 | tf_op jit(solution)/shard_map/all_to_all | solution.py:25
  38.3 22.6 %all-to-all-start.1 = ((bf16[64,4,2048]{2,1,0:T(4,128)(2,1)}), bf16[64,4,2048]{2,1,0:T(4,128)(2,1)S(1)}, u32[]{:S(2)}, u32[]{:S(2)}) async-start(bf16[64,4,2048]{2,1,0:T(4,128)(2,1)} %pad_maximum_fusion), calls=%async_computation.1 | async-start | bytes 2097152 | tf_op jit(solution)/shard_map/all_to_all | solution.py:25
  60.9 1.2 copy-start.3
  62.1 17.6 %all-to-all-start.2 = ((bf16[64,2,2048]{2,1,0:T(2,128)(2,1)}), bf16[64,2,2048]{2,1,0:T(2,128)(2,1)S(1)}, u32[]{:S(2)}, u32[]{:S(2)}) async-start(bf16[64,2,2048]{2,1,0:T(2,128)(2,1)} %broadcast_in_dim.23), calls=%async_computation.2 | async-start | bytes 1048576 | tf_op jit(solution)/shard_map/all_to_all | solution.py:25
  71.0 10.9 %copy-start.6 = (f32[2048]{0:T(1024)S(1)}, f32[2048]{0:T(1024)}, u32[]{:S(2)}) copy-start(f32[2048]{0:T(1024)} %param.16) | copy-start | bytes 24580
  71.0 24.3 %collective-permute-start.5 = (bf16[448,128]{1,0:T(8,128)(2,1)S(1)}, bf16[448,128]{1,0:T(8,128)(2,1)}, u32[]{:S(2)}, u32[]{:S(2)}) collective-permute-start(bf16[448,128]{1,0:T(8,128)(2,1)S(1)} %fusion.3), channel_id=1, source_target_pairs={{0,3},{1,0},{2,1},{3,2},{4,7},{5,4},{6,5},{7,6},{8,11},{9,8},{10,9... | collective-permute-start | bytes 344072 | tf_op jit(solution)/shard_map/ppermute | solution.py:84
  76.2 21.4 %collective-permute-start.4 = (bf16[448,128]{1,0:T(8,128)(2,1)S(1)}, bf16[448,128]{1,0:T(8,128)(2,1)}, u32[]{:S(2)}, u32[]{:S(2)}) collective-permute-start(bf16[448,128]{1,0:T(8,128)(2,1)S(1)} %fusion.3), channel_id=1, source_target_pairs={{0,2},{1,3},{2,0},{3,1},{4,6},{5,7},{6,4},{7,5},{8,10},{9,11},{10,... | collective-permute-start | bytes 344072 | tf_op jit(solution)/shard_map/ppermute | solution.py:84
  77.3 20.2 %collective-permute-start.3 = (bf16[448,128]{1,0:T(8,128)(2,1)S(1)}, bf16[448,128]{1,0:T(8,128)(2,1)}, u32[]{:S(2)}, u32[]{:S(2)}) collective-permute-start(bf16[448,128]{1,0:T(8,128)(2,1)S(1)} %fusion.3), channel_id=1, source_target_pairs={{0,1},{1,2},{2,3},{3,0},{4,5},{5,6},{6,7},{7,4},{8,9},{9,10},{10,1... | collective-permute-start | bytes 344072 | tf_op jit(solution)/shard_map/ppermute | solution.py:84
  79.7 0.8 copy-start.2
  88.1 27.3 %collective-permute-start.2 = (bf16[128,1024]{0,1:T(8,128)(2,1)S(1)}, bf16[128,1024]{0,1:T(8,128)(2,1)S(1)}, u32[]{:S(2)}, u32[]{:S(2)}) collective-permute-start(bf16[128,1024]{0,1:T(8,128)(2,1)S(1)} %concatenate.28), channel_id=1, source_target_pairs={{0,3},{1,0},{2,1},{3,2},{4,7},{5,4},{6,5},{7,6},{8,11},{9,8},{10,9... | collective-permute-start | bytes 786440 | tf_op jit(solution)/shard_map/ppermute | solution.py:108
  92.8 22.5 %collective-permute-start.1 = (bf16[128,1024]{0,1:T(8,128)(2,1)S(1)}, bf16[128,1024]{0,1:T(8,128)(2,1)S(1)}, u32[]{:S(2)}, u32[]{:S(2)}) collective-permute-start(bf16[128,1024]{0,1:T(8,128)(2,1)S(1)} %concatenate.28), channel_id=1, source_target_pairs={{0,2},{1,3},{2,0},{3,1},{4,6},{5,7},{6,4},{7,5},{8,10},{9,11},{10,... | collective-permute-start | bytes 786440 | tf_op jit(solution)/shard_map/ppermute | solution.py:108
  95.3 21.1 %collective-permute-start = (bf16[128,1024]{0,1:T(8,128)(2,1)S(1)}, bf16[128,1024]{0,1:T(8,128)(2,1)S(1)}, u32[]{:S(2)}, u32[]{:S(2)}) collective-permute-start(bf16[128,1024]{0,1:T(8,128)(2,1)S(1)} %concatenate.28), channel_id=1, source_target_pairs={{0,1},{1,2},{2,3},{3,0},{4,5},{5,6},{6,7},{7,4},{8,9},{9,10},{10,1... | collective-permute-start | bytes 786440 | tf_op jit(solution)/shard_map/ppermute | solution.py:108
  98.6 18.8 %copy-start.5 = (bf16[448,128]{1,0:T(8,128)(2,1)}, bf16[448,128]{1,0:T(8,128)(2,1)S(1)}, u32[]{:S(2)}) copy-start(bf16[448,128]{1,0:T(8,128)(2,1)S(1)} %get-tuple-element.17) | copy-start | bytes 344068
  98.6 29.0 %copy-start.8 = (s32[2]{0:T(128)S(1)}, s32[2]{0:T(128)}, u32[]{:S(2)}) copy-start(s32[2]{0:T(128)} %param.14) | copy-start | bytes 28
  98.6 37.5 %copy-start.7 = (s32[2]{0:T(128)S(1)}, s32[2]{0:T(128)}, u32[]{:S(2)}) copy-start(s32[2]{0:T(128)} %param.13) | copy-start | bytes 28
  116.5 32.9 %copy-start.4 = (f32[128,1024]{0,1:T(8,128)}, f32[128,1024]{0,1:T(8,128)S(1)}, u32[]{:S(2)}) copy-start(f32[128,1024]{0,1:T(8,128)S(1)} %convert_add_fusion) | copy-start | bytes 1572868
  117.4 18.4 %all-to-all-start.3 = ((f32[64,2,128]{2,1,0:T(2,128)}), f32[64,2,128]{2,1,0:T(2,128)S(1)}, u32[]{:S(2)}, u32[]{:S(2)}) async-start(f32[64,2,128]{2,1,0:T(2,128)} %bitcast.12), calls=%async_computation.3 | async-start | bytes 131072 | tf_op jit(solution)/shard_map/all_to_all | solution.py:25
  149.9 1.5 copy-start.1
  155.2 17.6 %all-to-all-start.5 = ((bf16[64,2,2176]{2,1,0:T(2,128)(2,1)}), bf16[64,2,2176]{2,1,0:T(2,128)(2,1)S(1)}, u32[]{:S(2)}, u32[]{:S(2)}) async-start(bf16[64,2,2176]{2,1,0:T(2,128)(2,1)} %concatenate.31), calls=%async_computation.5 | async-start | bytes 1114112 | tf_op jit(solution)/shard_map/all_to_all | solution.py:25

commit v2 on v1

v2 whole, which is shorter than its diff:
```python
import functools
import math

import jax
import jax.numpy as jnp
from jax import lax
from jax.experimental import pallas as pl
from jax.experimental.pallas import tpu as pltpu
from jax.sharding import PartitionSpec as P

D = 8192
EPS = 1e-05
BF = jnp.bfloat16
F32 = jnp.float32


def contract_last(left, right):
    return lax.dot_general(left, right, (((1,), (1,)), ((), ())), preferred_element_type=F32)


def gather_kernel(cols, ids_ref, low_ref, table_ref, extra_ref, out_ref, held, found, sems):
    rows = table_ref.shape[0]
    count = ids_ref.shape[0]
    low = low_ref[0]

    total = jnp.int32(0)
    for i in range(count):
        local = ids_ref[i] - low
        found[total] = i
        total = total + ((local >= 0) & (local < rows)).astype(jnp.int32)

    def copy(k):
        local = jnp.clip(ids_ref[found[k]] - low, 0, rows - 1)
        start = pl.multiple_of(lax.shift_left(lax.shift_right_logical(local, 3), 3), 8)
        return pltpu.make_async_copy(table_ref.at[pl.ds(start, 8), :], held.at[k], sems.at[k])

    def begin(k, carry):
        copy(k).start()
        return carry

    lax.fori_loop(0, total, begin, 0)
    extra = extra_ref[...]
    if extra.shape[1] == cols:
        out_ref[:, 2:4, :] = jnp.broadcast_to(extra[None], (count // 2, 2, cols))
    else:
        out_ref[:, :, cols:] = jnp.broadcast_to(extra[None], (count // 2, 2, extra.shape[1]))

    def finish(k, carry):
        copy(k).wait()
        i = found[k]
        local = ids_ref[i] - low
        row = lax.broadcasted_iota(jnp.int32, (8, cols), 0)
        wanted = jnp.where(row == (local & 7), held[k].astype(F32), 0.0)
        wanted = jnp.sum(wanted, axis=0, keepdims=True)
        which = lax.broadcasted_iota(jnp.int32, (2, cols), 0)
        pair = lax.shift_right_logical(i, 1)
        before = out_ref[pair, 0:2, 0:cols].astype(F32)
        out_ref[pair, 0:2, 0:cols] = jnp.where(which == (i & 1), wanted, before).astype(BF)
        return carry

    lax.fori_loop(0, total, finish, 0)


def gather_rows(ids, low, table, extra):
    count, cols = ids.shape[0], table.shape[1]
    block = (4, cols) if extra.shape[1] == cols else (2, cols + extra.shape[1])
    smem = pl.BlockSpec(memory_space=pltpu.SMEM)
    vmem = pl.BlockSpec(memory_space=pltpu.VMEM)
    table = pltpu.with_memory_space_constraint(table, pltpu.HBM)
    args = (ids, low, table, extra)
    return pl.pallas_call(
        functools.partial(gather_kernel, cols),
        out_shape=jax.ShapeDtypeStruct((count // 2,) + block, BF),
        in_specs=[smem, smem, pl.BlockSpec(memory_space=pltpu.HBM), vmem],
        out_specs=vmem,
        scratch_shapes=[
            pltpu.VMEM((count, 8, cols), BF),
            pltpu.SMEM((count + 1,), jnp.int32),
            pltpu.SemaphoreType.DMA((count,)),
        ],
        compiler_params=pltpu.CompilerParams(vmem_limit_bytes=16 << 20),
        cost_estimate=pl.CostEstimate(flops=0, transcendentals=0, bytes_accessed=1 << 20),
    )(*args)


def column(row, size):
    shape = (size, size)
    same = lax.broadcasted_iota(jnp.int32, shape, 0) == lax.broadcasted_iota(jnp.int32, shape, 1)
    return jnp.sum(jnp.where(same, row, 0.0), axis=1, keepdims=True)


def row_of(col, size):
    shape = (size, size)
    same = lax.broadcasted_iota(jnp.int32, shape, 0) == lax.broadcasted_iota(jnp.int32, shape, 1)
    return jnp.sum(jnp.where(same, col, 0.0), axis=0, keepdims=True)


def halves(value):
    high = value.astype(BF).astype(F32)
    return high, value - high


def forward_kernel(rows_ref, gain_ref, weight_ref, own_ref, probe_ref, out_ref):
    cols = rows_ref.shape[2]
    tokens = rows_ref.shape[0] * rows_ref.shape[1]
    rows = rows_ref[...].reshape(tokens, cols).astype(F32)
    scaled = (rows * gain_ref[...]).astype(BF)
    out_ref[0:tokens, :] = contract_last(scaled, weight_ref[...]).astype(BF)
    squares = row_of(jnp.sum(rows * rows, axis=1, keepdims=True), tokens)
    sq_high, sq_low = halves(squares)
    own_high, own_low = halves(contract_last(own_ref[...], probe_ref[...]))
    at = lax.broadcasted_iota(jnp.int32, (8, tokens), 0)
    side = jnp.zeros((8, tokens), F32)
    lines = [sq_high, sq_low, own_high[0:1], own_high[1:2], own_low[0:1], own_low[1:2]]
    for i, line in enumerate(lines):
        side = jnp.where(at == i, line, side)
    out_ref[tokens:, 0:tokens] = side.astype(BF)
    out_ref[tokens:, tokens:] = jnp.zeros((8, out_ref.shape[1] - tokens), BF)


def middle_kernel(tokens, sums_ref, *rest):
    down_refs, (logit_ref, gate_up_ref, inv_ref, side_ref, down_ref) = rest[:-5], rest[-5:]
    block = tokens + 8
    total = sums_ref[0:block, :].astype(F32)
    for k in range(1, sums_ref.shape[0] // block):
        total = total + sums_ref[k * block : (k + 1) * block, :].astype(F32)
    side = total[tokens:, 0:tokens]
    side_ref[...] = side
    inv = lax.rsqrt(column(side[0:1] + side[1:2], tokens) / D + EPS)
    inv_ref[...] = jnp.broadcast_to(inv, (tokens, 128))
    gate_up = total[0:tokens] * inv
    gate_up_ref[...] = gate_up
    main = gate_up.shape[1] // 2 - 64
    gate, shared, up = gate_up[:, :main], gate_up[:, main : main + 128], gate_up[:, main + 128 :]
    hidden = gate * jax.nn.sigmoid(gate) * up
    lane = lax.broadcasted_iota(jnp.int32, shared.shape, 1)
    tail = jnp.where(lane < 64, shared * jax.nn.sigmoid(shared) * pltpu.roll(shared, 64, 1), 0.0)
    hidden = jnp.concatenate([hidden, tail], axis=1).astype(BF)
    down = down_refs[0][...].astype(F32)
    for ref in down_refs[1:]:
        down = down + ref[...].astype(F32)
    high, low = halves(down)
    down_ref[...] = high.astype(BF)
    pad = jnp.zeros((64, high.shape[1]), BF)
    high = jnp.concatenate([high.astype(BF), pad], axis=0)
    low = jnp.concatenate([low.astype(BF), pad], axis=0)
    logit_ref[...] = jnp.dot(hidden, high, preferred_element_type=F32) + jnp.dot(
        hidden, low, preferred_element_type=F32
    )


def backward_kernel(grad_ref, down_ref, gate_up_ref, weight_ref, out_ref):
    cols = weight_ref.shape[1]
    gate_up = gate_up_ref[...]
    main = gate_up.shape[1] // 2 - 64
    gate, shared, up = gate_up[:, :main], gate_up[:, main : main + 128], gate_up[:, main + 128 :]
    down = down_ref[...]
    down = jnp.concatenate([down, jnp.zeros((64, down.shape[1]), BF)], axis=0)
    hidden_grad = contract_last(grad_ref[...], down)

    def both(grad, gate, up):
        sig = jax.nn.sigmoid(gate)
        return grad * up * sig * (1.0 + gate * (1.0 - sig)), grad * gate * sig

    gate_grad, up_grad = both(hidden_grad[:, :main], gate, up)
    tail_gate, tail_up = both(hidden_grad[:, main:], shared, pltpu.roll(shared, 64, 1))
    lane = lax.broadcasted_iota(jnp.int32, shared.shape, 1)
    tail = jnp.where(lane < 64, tail_gate, pltpu.roll(tail_up, 64, 1))
    grads = jnp.concatenate([gate_grad, tail, up_grad], axis=1).astype(BF)
    normed = jnp.dot(grads, weight_ref[...], preferred_element_type=F32)
    shape = out_ref.shape[:2]
    out_ref[:, :, 0:cols] = normed.astype(BF).reshape(shape + (cols,))
    inner = jnp.sum(grads.astype(F32) * gate_up, axis=1, keepdims=True)
    high, low = halves(inner)
    pair = jnp.where(lane == 0, high, jnp.where(lane == 1, low, 0.0))
    out_ref[:, :, cols:] = pair.astype(BF).reshape(shape + (128,))


def on_core(kernel, out_shape, *args, flops=0):
    return pl.pallas_call(
        kernel,
        out_shape=out_shape,
        compiler_params=pltpu.CompilerParams(vmem_limit_bytes=24 << 20),
        cost_estimate=pl.CostEstimate(flops=flops, transcendentals=0, bytes_accessed=5 << 20),
    )(*args)


def swap(blocks):
    return lax.all_to_all(blocks, "wide", 0, 0, tiled=True)


def body(token_ids, attr_ids, target, loss_mask, embed_table, norm_gain, w_gate, w_up, w_down):
    wide = lax.axis_size("wide")
    narrow = lax.axis_size("narrow")
    my_wide = lax.axis_index("wide")
    tok_dev = token_ids.shape[0]
    tokens = tok_dev * wide
    attrs = attr_ids.shape[0]
    vocab_rows, cols = embed_table.shape
    ff = w_gate.shape[1]
    logit_scale = 3.0 / math.sqrt(D)

    def pick(received, ids):
        owner = ids // vocab_rows
        return jnp.concatenate(
            [
                lax.dynamic_slice(received, (owner[i], i, 0), (1, 1, cols)).reshape(1, cols)
                for i in range(tok_dev)
            ],
            axis=0,
        )

    main = ff // 128 * 128
    weight = jnp.concatenate([w_gate.T, w_up.T[main:], w_up.T[:main]], axis=0)

    ids_high = (token_ids // 256).astype(BF)
    ids_low = (token_ids % 256).astype(BF)
    extra = jnp.stack([ids_high, ids_low], axis=1)
    extra = jnp.pad(extra, ((0, 0), (0, 126)))
    low = (my_wide * vocab_rows).reshape(1)
    first = swap(gather_rows(attr_ids, low, embed_table, extra))
    digits = first[:, :, cols : cols + 2].astype(F32)
    all_ids = (digits[:, :, 0] * 256.0 + digits[:, :, 1]).astype(jnp.int32).reshape(tokens)
    my_attrs = lax.dynamic_slice_in_dim(attr_ids, my_wide * tok_dev, tok_dev, 0)
    probe_own, weight = lax.optimization_barrier((pick(first, my_attrs), weight))

    second = swap(gather_rows(all_ids, low, embed_table, probe_own))
    probe = second[:, tok_dev:, :].reshape(attrs, cols)
    rows_own = pick(second, token_ids)
    rows = swap(jnp.broadcast_to(rows_own[None], (wide, tok_dev, cols)))

    down_part = contract_last(w_down, probe).astype(BF)
    down_parts = [down_part]
    for step in range(1, narrow):
        pairs = [(i, (i + step) % narrow) for i in range(narrow)]
        down_parts.append(lax.ppermute(down_part, "narrow", pairs))

    part = on_core(
        forward_kernel,
        jax.ShapeDtypeStruct((tokens + 8, 2 * ff), BF),
        rows,
        norm_gain.reshape(1, cols),
        weight,
        rows_own,
        probe,
        flops=4 * tokens * cols * ff,
    )
    sums = lax.all_gather(part, "narrow", axis=0, tiled=True)
    logit_part, gate_up, inv_all, side, down_probe = on_core(
        functools.partial(middle_kernel, tokens),
        (
            jax.ShapeDtypeStruct((tokens, attrs), F32),
            jax.ShapeDtypeStruct((tokens, 2 * ff), F32),
            jax.ShapeDtypeStruct((tokens, 128), F32),
            jax.ShapeDtypeStruct((8, attrs), F32),
            jax.ShapeDtypeStruct((ff, attrs), BF),
        ),
        sums,
        *down_parts,
        flops=4 * tokens * ff * attrs,
    )
    own_logits = side[2:4] + side[4:6]
    inv_own = lax.dynamic_slice_in_dim(inv_all, my_wide * tok_dev, tok_dev, 0)[:, :1]

    logit_sum = jnp.sum(swap(logit_part.reshape(wide, tok_dev, attrs)), axis=0)
    logits = (logit_sum + own_logits) * logit_scale
    probability = jax.nn.softmax(logits, axis=1)
    onehot = (target[:, None] == jnp.arange(attrs, dtype=jnp.int32)[None, :]).astype(F32)
    grad_own = ((probability - onehot) * loss_mask[:, None].astype(F32)).astype(BF)
    logit_grad = swap(jnp.broadcast_to(grad_own[None], (wide, tok_dev, attrs))).reshape(
        tokens, attrs
    )
    out_grad = jnp.dot(grad_own, probe, preferred_element_type=F32)

    last = on_core(
        backward_kernel,
        jax.ShapeDtypeStruct((wide, tok_dev, cols + 128), BF),
        logit_grad,
        down_probe,
        gate_up,
        weight,
        flops=4 * tokens * cols * ff,
    )
    last = swap(last)
    last = jnp.sum(last.astype(F32), axis=0)
    scaled = last[:, :cols] * norm_gain
    inner = last[:, cols : cols + 1] + last[:, cols + 1 : cols + 2]
    result = out_grad + inv_own * scaled - rows_own.astype(F32) * (inv_own * inv_own * inner / D)
    return result.astype(BF)


def solution(mesh):
    return jax.shard_map(
        body,
        mesh=mesh,
        in_specs=(
            P("wide"),
            P(),
            P("wide"),
            P("wide"),
            P("wide", "narrow"),
            P("narrow"),
            P("narrow", "wide"),
            P("narrow", "wide"),
            P("wide", "narrow"),
        ),
        out_specs=P("wide", "narrow"),
        check_vma=False,
    )
```

time: 175 us -> 161 us (0.920)
  waiting for transfers between devices: 60.1 us -> 36.6 us
  blocking collectives: 11.9 us -> 34 us
  Pallas kernels: 0 us -> 11.8 us
  local copies, waits for them, and re-layouts: 22.9 us -> 14.3 us
  matrix products: 9.66 us -> 1.44 us
  starting transfers between devices: 52.5 us -> 47 us
  other arithmetic: 9.54 us -> 7.45 us
    all_gather x0 -> x1, blocking collectives: none -> 22 us  [body(): sums = lax.all_gather(part, 'narrow', axis=0, tiled=True)]
    ppermute x6 -> x3, waiting for transfers between devices: 17.7 us -> 0.01 us  [body(): down_parts.append(lax.ppermute(down_part, 'narrow', pairs))]
    pallas_call x0 -> x5, Pallas kernels: none -> 11.8 us  [the longest x2 7.53 us: gather_rows(): pl.pallas_call(functools.partial(gather_kernel, cols), out_shape=jax.Shap...]
    gather x2 -> x0, local copies, waits for them, and re-layouts: 8.34 us -> none  [rows_here(): return jnp.take(embed_table, local, axis=0)]
    ppermute x6 -> x3, starting transfers between devices: 17.9 us -> 9.67 us  [body(): down_parts.append(lax.ppermute(down_part, 'narrow', pairs))]
    all_to_all x5, waiting for transfers between devices: 42.4 us -> 36.6 us  [swap(): return lax.all_to_all(blocks, 'wide', 0, 0, tiled=True)]
    concatenate x3 -> x0, local copies, waits for them, and re-layouts: 5.44 us -> none  [the longest x2 3.31 us: body(): jnp.concatenate([normed_part.astype(BF), inner_high, inner_low, jnp.zeros...]
    dot_general x3 -> x0, matrix products: 4.38 us -> none  [the longest x1 2.81 us: body(): up_part = jnp.dot(scaled_rows, w_up, preferred_element_type=F32)]
  transfers between devices with their start and end apart: 11 -> 8, of which waited for: 6 -> 5; matrix products, arithmetic and copies ran while one was open for 9% -> 6% of each run, Pallas kernels for 0% -> 1%
where the time goes in v2:
time: 161 us; the launch traced here: 160 us
  starting transfers between devices  47 us (29%)
  waiting for transfers between devices  36.6 us (23%)
  blocking collectives  34 us (21%)
  local copies, waits for them, and re-layouts  14.3 us (9%)
  Pallas kernels  11.8 us (7%)
  between operations  7.58 us (5%)
  other arithmetic  7.45 us (5%)
    all_to_all x5, starting transfers between devices, swap(): return lax.all_to_all(blocks, 'wide', 0, 0, tiled=True)  37.3 us
    all_to_all x5, waiting for transfers between devices, swap(): return lax.all_to_all(blocks, 'wide', 0, 0, tiled=True)  36.6 us
    all_gather x1, blocking collectives, body(): sums = lax.all_gather(part, 'narrow', axis=0, tiled=True)  22 us
    all_to_all x1, blocking collectives, swap(): return lax.all_to_all(blocks, 'wide', 0, 0, tiled=True)  11.9 us
    ppermute x3, starting transfers between devices, body(): down_parts.append(lax.ppermute(down_part, 'narrow', pairs))  9.67 us
    pallas_call x2, Pallas kernels, gather_rows(): pl.pallas_call(functools.partial(gather_kernel, cols), out_shape=jax.Shap...  7.53 us
    unnamed x18, local copies, waits for them, and re-layouts  5.74 us
    pallas_call x3, Pallas kernels, on_core(): pl.pallas_call(kernel, out_shape=out_shape, compiler_params=pltpu.Compile...  4.29 us
  transfers between devices with their start and end apart: 8, of which 5 were waited for; matrix products, arithmetic and copies ran while one was open for 6% of the time, Pallas kernels for 1%

profile of v2, /device:TPU:1, one launch (start us, length us, event | category | flops | bytes accessed | tf_op | source)
XLA Modules:
  0.0 160.1 jit_solution(2773854488983256447)
XLA Ops:
  1.8 3.7 %shard_map.91 = bf16[64,2,2176]{2,1,0:T(2,128)(2,1)} custom-call(s32[128]{0:T(128)S(1)} %copy-done.4, s32[1]{0:T(128)} %bitcast.low_ref, bf16[1024,2048]{1,0:T(8,128)(2,1)} %table_ref.3, bf16[2,128]{1,0:T(2,128)(2,1)S(1)} %fusion.12.extra_ref), custom_call_target="tpu_custom_call" | custom-call | bytes 1048576 | tf_op jit(solution)/shard_map/pallas_call | solution.py:71
  5.4 10.6 %all-to-all-start = ((bf16[64,2,2176]{2,1,0:T(2,128)(2,1)}), bf16[64,2,2176]{2,1,0:T(2,128)(2,1)}, u32[]{:S(2)}, u32[]{:S(2)}) async-start(bf16[64,2,2176]{2,1,0:T(2,128)(2,1)} %shard_map.91), calls=%async_computation | async-start | bytes 1114112 | tf_op jit(solution)/shard_map/all_to_all | solution.py:189
  19.2 1.5 slice.68
  20.8 1.7 %slice.67 = bf16[64,2048]{1,0:T(8,128)(2,1)} slice(bf16[448,2048]{1,0:T(8,128)(2,1)} %bitcast.32), slice={[384:448], [0:2048]} | slice | bytes 524288 | tf_op jit(solution)/shard_map/slice | solution.py:214
  23.7 3.3 %pad_maximum_fusion.weight_ref = bf16[896,2048]{1,0:T(8,128)(2,1)} fusion(bf16[384,2048]{1,0:T(8,128)(2,1)S(1)} %slice.68, bf16[64,2048]{1,0:T(8,128)(2,1)} %slice.67, bf16[448,2048]{1,0:T(8,128)(2,1)} %bitcast.30), kind=kLoop, calls=%fused_computation | loop fusion | flops 11010048 | bytes 7340032 | tf_op jit(solution)/shard_map/concatenate | solution.py:214
  27.0 1.7 %all-to-all-done = bf16[64,2,2176]{2,1,0:T(2,128)(2,1)} async-done(((bf16[64,2,2176]{2,1,0:T(2,128)(2,1)}), bf16[64,2,2176]{2,1,0:T(2,128)(2,1)}, u32[]{:S(2)}, u32[]{:S(2)}) %all-to-all-start) | async-done | bytes 557088 | tf_op jit(solution)/shard_map/all_to_all | solution.py:189
  31.7 3.9 %shard_map.92 = bf16[64,4,2048]{2,1,0:T(4,128)(2,1)} custom-call(s32[128]{0:T(128)S(1)} %convert_element_type.46.ids_ref, s32[1]{0:T(128)} %bitcast.low_ref, bf16[1024,2048]{1,0:T(8,128)(2,1)} %table_ref.3, bf16[2,2048]{1,0:T(2,128)(2,1)S(1)} %pad_maximum_fusion.1.extra_ref), custom_call_target="tpu_custom_call" | custom-call | bytes 1048576 | tf_op jit(solution)/shard_map/pallas_call | solution.py:71
  35.5 7.2 %all-to-all-start.1 = ((bf16[64,4,2048]{2,1,0:T(4,128)(2,1)}), bf16[64,4,2048]{2,1,0:T(4,128)(2,1)S(1)}, u32[]{:S(2)}, u32[]{:S(2)}) async-start(bf16[64,4,2048]{2,1,0:T(4,128)(2,1)} %shard_map.92), calls=%async_computation.1 | async-start | bytes 2097152 | tf_op jit(solution)/shard_map/all_to_all | solution.py:189
  46.9 13.8 %all-to-all-done.1 = bf16[64,4,2048]{2,1,0:T(4,128)(2,1)S(1)} async-done(((bf16[64,4,2048]{2,1,0:T(4,128)(2,1)}), bf16[64,4,2048]{2,1,0:T(4,128)(2,1)S(1)}, u32[]{:S(2)}, u32[]{:S(2)}) %all-to-all-start.1) | async-done | bytes 1048608 | tf_op jit(solution)/shard_map/all_to_all | solution.py:189
  62.8 4.7 %all-to-all-start.2 = ((bf16[64,2,2048]{2,1,0:T(2,128)(2,1)}), bf16[64,2,2048]{2,1,0:T(2,128)(2,1)S(1)}, u32[]{:S(2)}, u32[]{:S(2)}) async-start(bf16[64,2,2048]{2,1,0:T(2,128)(2,1)} %broadcast_in_dim.4), calls=%async_computation.2 | async-start | bytes 1048576 | tf_op jit(solution)/shard_map/all_to_all | solution.py:189
  67.4 1.8 %slice.69 = bf16[64,2,2048]{2,1,0:T(2,128)(2,1)S(1)} slice(bf16[64,4,2048]{2,1,0:T(4,128)(2,1)} %copy-done.6), slice={[0:64], [2:4], [0:2048]} | slice | bytes 1048576 | tf_op jit(solution)/shard_map/slice | solution.py:228
  70.1 3.1 %collective-permute-start = (bf16[448,128]{1,0:T(8,128)(2,1)S(1)}, bf16[448,128]{1,0:T(8,128)(2,1)S(1)}, u32[]{:S(2)}, u32[]{:S(2)}) collective-permute-start(bf16[448,128]{1,0:T(8,128)(2,1)S(1)} %fusion.2.rest_0_), channel_id=1, source_target_pairs={{0,1},{1,2},{2,3},{3,0},{4,5},{5,6},{6,7},{7,4},{8,9},{9,10},{10,1... | collective-permute-start | bytes 344072 | tf_op jit(solution)/shard_map/ppermute | solution.py:236
  73.2 4.2 %collective-permute-start.1 = (bf16[448,128]{1,0:T(8,128)(2,1)S(1)}, bf16[448,128]{1,0:T(8,128)(2,1)S(1)}, u32[]{:S(2)}, u32[]{:S(2)}) collective-permute-start(bf16[448,128]{1,0:T(8,128)(2,1)S(1)} %fusion.2.rest_0_), channel_id=1, source_target_pairs={{0,2},{1,3},{2,0},{3,1},{4,6},{5,7},{6,4},{7,5},{8,10},{9,11},{10,... | collective-permute-start | bytes 344072 | tf_op jit(solution)/shard_map/ppermute | solution.py:236
  77.4 2.4 %collective-permute-start.2 = (bf16[448,128]{1,0:T(8,128)(2,1)S(1)}, bf16[448,128]{1,0:T(8,128)(2,1)S(1)}, u32[]{:S(2)}, u32[]{:S(2)}) collective-permute-start(bf16[448,128]{1,0:T(8,128)(2,1)S(1)} %fusion.2.rest_0_), channel_id=1, source_target_pairs={{0,3},{1,0},{2,1},{3,2},{4,7},{5,4},{6,5},{7,6},{8,11},{9,8},{10,9... | collective-permute-start | bytes 344072 | tf_op jit(solution)/shard_map/ppermute | solution.py:236
  79.9 2.0 %copy-done.1 = bf16[896,2048]{1,0:T(8,128)(2,1)S(1)} copy-done((bf16[896,2048]{1,0:T(8,128)(2,1)S(1)}, bf16[896,2048]{1,0:T(8,128)(2,1)}, u32[]{:S(2)}) %copy-start.1) | copy-done | bytes 3670040
  81.9 1.5 shard_map.93
  83.4 22.0 %all_gather.3.sums_ref = bf16[544,896]{1,0:T(8,128)(2,1)S(1)} all-gather(bf16[136,896]{1,0:T(8,128)(2,1)S(1)} %shard_map.93), channel_id=1, replica_groups=mesh['wide'=64,'narrow'=4] {'narrow'}, dimensions={0}, use_global_device_ids=true | all-gather | bytes 1218560 | tf_op jit(solution)/shard_map/all_gather | solution.py:248
  106.5 10.2 %all-to-all-start.3 = ((f32[64,2,128]{2,1,0:T(2,128)}), f32[64,2,128]{2,1,0:T(2,128)S(1)}, u32[]{:S(2)}, u32[]{:S(2)}) async-start(f32[64,2,128]{2,1,0:T(2,128)} %bitcast.15), calls=%async_computation.3 | async-start | bytes 131072 | tf_op jit(solution)/shard_map/all_to_all | solution.py:189
  116.7 8.1 %all-to-all-done.3 = f32[64,2,128]{2,1,0:T(2,128)S(1)} async-done(((f32[64,2,128]{2,1,0:T(2,128)}), f32[64,2,128]{2,1,0:T(2,128)S(1)}, u32[]{:S(2)}, u32[]{:S(2)}) %all-to-all-start.3) | async-done | bytes 65568 | tf_op jit(solution)/shard_map/all_to_all | solution.py:189
  125.3 11.9 %all_to_all.30 = bf16[64,2,128]{2,1,0:T(2,128)(2,1)S(1)} all-to-all(bf16[64,2,128]{2,1,0:T(2,128)(2,1)S(1)} %broadcast_in_dim.5), channel_id=1, replica_groups=mesh['wide'=64,'narrow'=4] {'wide'}, dimensions={0} | all-to-all | bytes 65536 | tf_op jit(solution)/shard_map/all_to_all | solution.py:189
  137.2 2.0 %copy-done.2 = bf16[896,2048]{1,0:T(8,128)(2,1)S(1)} copy-done((bf16[896,2048]{1,0:T(8,128)(2,1)S(1)}, bf16[896,2048]{1,0:T(8,128)(2,1)}, u32[]{:S(2)}) %copy-start.2) | copy-done | bytes 3670040
  139.3 1.8 %shard_map.95 = bf16[64,2,2176]{2,1,0:T(2,128)(2,1)} custom-call(bf16[128,128]{1,0:T(8,128)(2,1)S(1)} %bitcast.28, bf16[448,128]{1,0:T(8,128)(2,1)S(1)} %get-tuple-element.17.down_ref, f32[128,896]{1,0:T(8,128)S(1)} %get-tuple-element.18.gate_up_ref, bf16[896,2048]{1,0:T(8,128)(2,1)S(1)} %copy-done.2), custom_call_target="tpu_custom_call" | custom-call | flops 469762048 | bytes 5242880 | tf_op jit(solution)/shard_map/pallas_call | solution.py:180
  141.0 4.7 %all-to-all-start.5 = ((bf16[64,2,2176]{2,1,0:T(2,128)(2,1)}), bf16[64,2,2176]{2,1,0:T(2,128)(2,1)S(1)}, u32[]{:S(2)}, u32[]{:S(2)}) async-start(bf16[64,2,2176]{2,1,0:T(2,128)(2,1)} %shard_map.95), calls=%async_computation.5 | async-start | bytes 1114112 | tf_op jit(solution)/shard_map/all_to_all | solution.py:189
  145.8 12.9 %all-to-all-done.5 = bf16[64,2,2176]{2,1,0:T(2,128)(2,1)S(1)} async-done(((bf16[64,2,2176]{2,1,0:T(2,128)(2,1)}), bf16[64,2,2176]{2,1,0:T(2,128)(2,1)S(1)}, u32[]{:S(2)}, u32[]{:S(2)}) %all-to-all-start.5) | async-done | bytes 557088 | tf_op jit(solution)/shard_map/all_to_all | solution.py:189
  (48 shorter events, 12.0 us)
Async XLA Ops:
  0.0 69.5 %copy-start = (bf16[448,2048]{1,0:T(8,128)(2,1)S(1)}, bf16[448,2048]{1,0:T(8,128)(2,1)}, u32[]{:S(2)}) copy-start(bf16[448,2048]{1,0:T(8,128)(2,1)} %param.17) | copy-start | bytes 5505028
  0.0 16.0 %copy-start.5 = (s32[128]{0:T(128)S(1)}, s32[128]{0:T(128)}, u32[]{:S(2)}) copy-start(s32[128]{0:T(128)} %ids_ref.1) | copy-start | bytes 1540
  1.1 0.7 copy-start.4
  5.4 23.3 %all-to-all-start = ((bf16[64,2,2176]{2,1,0:T(2,128)(2,1)}), bf16[64,2,2176]{2,1,0:T(2,128)(2,1)}, u32[]{:S(2)}, u32[]{:S(2)}) async-start(bf16[64,2,2176]{2,1,0:T(2,128)(2,1)} %shard_map.91), calls=%async_computation | async-start | bytes 1114112 | tf_op jit(solution)/shard_map/all_to_all | solution.py:189
  35.5 44.4 %copy-start.3 = (f32[2048]{0:T(1024)S(1)}, f32[2048]{0:T(1024)}, u32[]{:S(2)}) copy-start(f32[2048]{0:T(1024)} %param.14) | copy-start | bytes 24580
  35.5 25.1 %all-to-all-start.1 = ((bf16[64,4,2048]{2,1,0:T(4,128)(2,1)}), bf16[64,4,2048]{2,1,0:T(4,128)(2,1)S(1)}, u32[]{:S(2)}, u32[]{:S(2)}) async-start(bf16[64,4,2048]{2,1,0:T(4,128)(2,1)} %shard_map.92), calls=%async_computation.1 | async-start | bytes 2097152 | tf_op jit(solution)/shard_map/all_to_all | solution.py:189
  60.7 1.0 copy-start.6
  62.8 17.1 %all-to-all-start.2 = ((bf16[64,2,2048]{2,1,0:T(2,128)(2,1)}), bf16[64,2,2048]{2,1,0:T(2,128)(2,1)S(1)}, u32[]{:S(2)}, u32[]{:S(2)}) async-start(bf16[64,2,2048]{2,1,0:T(2,128)(2,1)} %broadcast_in_dim.4), calls=%async_computation.2 | async-start | bytes 1048576 | tf_op jit(solution)/shard_map/all_to_all | solution.py:189
  70.1 35.3 %collective-permute-start = (bf16[448,128]{1,0:T(8,128)(2,1)S(1)}, bf16[448,128]{1,0:T(8,128)(2,1)S(1)}, u32[]{:S(2)}, u32[]{:S(2)}) collective-permute-start(bf16[448,128]{1,0:T(8,128)(2,1)S(1)} %fusion.2.rest_0_), channel_id=1, source_target_pairs={{0,1},{1,2},{2,3},{3,0},{4,5},{5,6},{6,7},{7,4},{8,9},{9,10},{10,1... | collective-permute-start | bytes 344072 | tf_op jit(solution)/shard_map/ppermute | solution.py:236
  73.2 32.3 %collective-permute-start.1 = (bf16[448,128]{1,0:T(8,128)(2,1)S(1)}, bf16[448,128]{1,0:T(8,128)(2,1)S(1)}, u32[]{:S(2)}, u32[]{:S(2)}) collective-permute-start(bf16[448,128]{1,0:T(8,128)(2,1)S(1)} %fusion.2.rest_0_), channel_id=1, source_target_pairs={{0,2},{1,3},{2,0},{3,1},{4,6},{5,7},{6,4},{7,5},{8,10},{9,11},{10,... | collective-permute-start | bytes 344072 | tf_op jit(solution)/shard_map/ppermute | solution.py:236
  77.4 28.1 %collective-permute-start.2 = (bf16[448,128]{1,0:T(8,128)(2,1)S(1)}, bf16[448,128]{1,0:T(8,128)(2,1)S(1)}, u32[]{:S(2)}, u32[]{:S(2)}) collective-permute-start(bf16[448,128]{1,0:T(8,128)(2,1)S(1)} %fusion.2.rest_0_), channel_id=1, source_target_pairs={{0,3},{1,0},{2,1},{3,2},{4,7},{5,4},{6,5},{7,6},{8,11},{9,8},{10,9... | collective-permute-start | bytes 344072 | tf_op jit(solution)/shard_map/ppermute | solution.py:236
  79.9 2.0 %copy-start.1 = (bf16[896,2048]{1,0:T(8,128)(2,1)S(1)}, bf16[896,2048]{1,0:T(8,128)(2,1)}, u32[]{:S(2)}) copy-start(bf16[896,2048]{1,0:T(8,128)(2,1)} %pad_maximum_fusion.weight_ref) | copy-start | bytes 11010052
  81.9 34.8 %copy-start.8 = (s32[2]{0:T(128)S(1)}, s32[2]{0:T(128)}, u32[]{:S(2)}) copy-start(s32[2]{0:T(128)} %param.12) | copy-start | bytes 28
  81.9 43.2 %copy-start.7 = (s32[2]{0:T(128)S(1)}, s32[2]{0:T(128)}, u32[]{:S(2)}) copy-start(s32[2]{0:T(128)} %param.11) | copy-start | bytes 28
  106.5 18.3 %all-to-all-start.3 = ((f32[64,2,128]{2,1,0:T(2,128)}), f32[64,2,128]{2,1,0:T(2,128)S(1)}, u32[]{:S(2)}, u32[]{:S(2)}) async-start(f32[64,2,128]{2,1,0:T(2,128)} %bitcast.15), calls=%async_computation.3 | async-start | bytes 131072 | tf_op jit(solution)/shard_map/all_to_all | solution.py:189
  137.2 2.0 %copy-start.2 = (bf16[896,2048]{1,0:T(8,128)(2,1)S(1)}, bf16[896,2048]{1,0:T(8,128)(2,1)}, u32[]{:S(2)}) copy-start(bf16[896,2048]{1,0:T(8,128)(2,1)} %pad_maximum_fusion.weight_ref) | copy-start | bytes 11010052
  141.0 17.6 %all-to-all-start.5 = ((bf16[64,2,2176]{2,1,0:T(2,128)(2,1)}), bf16[64,2,2176]{2,1,0:T(2,128)(2,1)S(1)}, u32[]{:S(2)}, u32[]{:S(2)}) async-start(bf16[64,2,2176]{2,1,0:T(2,128)(2,1)} %shard_map.95), calls=%async_computation.5 | async-start | bytes 1114112 | tf_op jit(solution)/shard_map/all_to_all | solution.py:189

commit v3 on v2

--- a/solution.py
+++ b/solution.py
@@ -18,39 +18,54 @@
     return lax.dot_general(left, right, (((1,), (1,)), ((), ())), preferred_element_type=F32)
 
 
-def gather_kernel(cols, ids_ref, low_ref, table_ref, extra_ref, out_ref, held, found, sems):
-    rows = table_ref.shape[0]
-    count = ids_ref.shape[0]
-    low = low_ref[0]
-
-    total = jnp.int32(0)
-    for i in range(count):
-        local = ids_ref[i] - low
-        found[total] = i
-        total = total + ((local >= 0) & (local < rows)).astype(jnp.int32)
+def column(row, size):
+    shape = (size, size)
+    same = lax.broadcasted_iota(jnp.int32, shape, 0) == lax.broadcasted_iota(jnp.int32, shape, 1)
+    return jnp.sum(jnp.where(same, row, 0.0), axis=1, keepdims=True)
+
+
+def row_of(col, size):
+    shape = (size, size)
+    same = lax.broadcasted_iota(jnp.int32, shape, 0) == lax.broadcasted_iota(jnp.int32, shape, 1)
+    return jnp.sum(jnp.where(same, col, 0.0), axis=0, keepdims=True)
+
+
+def collect(ids, low, table_ref, out_ref, held, sems, meta_ref, meta_sem, list_ref):
+    rows, cols = table_ref.shape
+    count = ids.shape[0]
+    local = ids - low.astype(F32)
+    mine = jnp.where((local >= 0.0) & (local < float(rows)), 1.0, 0.0)
+    at = lax.broadcasted_iota(jnp.int32, (count, count), 0)
+    slot = lax.broadcasted_iota(jnp.int32, (count, count), 1)
+    ahead = jnp.sum(jnp.where(slot < at, row_of(mine, count), 0.0), axis=1, keepdims=True)
+    chosen = slot.astype(F32) == jnp.broadcast_to(jnp.where(mine > 0.0, ahead, -1.0), (count, count))
+    which = jnp.sum(jnp.where(chosen, at.astype(F32), 0.0), axis=0, keepdims=True)
+    place = jnp.sum(jnp.where(chosen, local, 0.0), axis=0, keepdims=True)
+    total = jnp.sum(jnp.broadcast_to(mine, (count, count)), axis=0, keepdims=True)
+    line = lax.broadcasted_iota(jnp.int32, (8, count), 0)
+    meta = jnp.where(line == 0, which, jnp.where(line == 1, place, total))
+    meta_ref[...] = meta.astype(jnp.int32)
+    to_scalars = pltpu.make_async_copy(meta_ref, list_ref, meta_sem)
+    to_scalars.start()
+    to_scalars.wait()
 
     def copy(k):
-        local = jnp.clip(ids_ref[found[k]] - low, 0, rows - 1)
-        start = pl.multiple_of(lax.shift_left(lax.shift_right_logical(local, 3), 3), 8)
-        return pltpu.make_async_copy(table_ref.at[pl.ds(start, 8), :], held.at[k], sems.at[k])
+        first = lax.shift_left(lax.shift_right_logical(list_ref[1, k], 3), 3)
+        return pltpu.make_async_copy(
+            table_ref.at[pl.ds(pl.multiple_of(first, 8), 8), :], held.at[k], sems.at[k]
+        )
 
     def begin(k, carry):
         copy(k).start()
         return carry
 
-    lax.fori_loop(0, total, begin, 0)
-    extra = extra_ref[...]
-    if extra.shape[1] == cols:
-        out_ref[:, 2:4, :] = jnp.broadcast_to(extra[None], (count // 2, 2, cols))
-    else:
-        out_ref[:, :, cols:] = jnp.broadcast_to(extra[None], (count // 2, 2, extra.shape[1]))
-
-    def finish(k, carry):
+    lax.fori_loop(0, list_ref[2, 0], begin, 0)
+
+    def put(k, carry):
         copy(k).wait()
-        i = found[k]
-        local = ids_ref[i] - low
+        i = list_ref[0, k]
         row = lax.broadcasted_iota(jnp.int32, (8, cols), 0)
-        wanted = jnp.where(row == (local & 7), held[k].astype(F32), 0.0)
+        wanted = jnp.where(row == (list_ref[1, k] & 7), held[k].astype(F32), 0.0)
         wanted = jnp.sum(wanted, axis=0, keepdims=True)
         which = lax.broadcasted_iota(jnp.int32, (2, cols), 0)
         pair = lax.shift_right_logical(i, 1)
@@ -58,41 +73,78 @@
         out_ref[pair, 0:2, 0:cols] = jnp.where(which == (i & 1), wanted, before).astype(BF)
         return carry
 
-    lax.fori_loop(0, total, finish, 0)
-
-
-def gather_rows(ids, low, table, extra):
-    count, cols = ids.shape[0], table.shape[1]
-    block = (4, cols) if extra.shape[1] == cols else (2, cols + extra.shape[1])
+    return lambda: lax.fori_loop(0, list_ref[2, 0], put, 0)
+
+
+def pick(blocks_ref, ids, cols):
+    which = lax.broadcasted_iota(jnp.int32, (2, cols), 0)
+    blocks = [blocks_ref[owner, 0:2, 0:cols].astype(F32) for owner in ids]
+    return jnp.where(which == 0, blocks[0], blocks[1]).astype(BF)
+
+
+def first_kernel(low_ref, token_ref, ids_ref, table_ref, out_ref, *scratch):
+    cols = table_ref.shape[1]
+    count = ids_ref.shape[1]
+    ids = column(ids_ref[...].astype(F32), count)
+    finish = collect(ids, low_ref[0], table_ref, out_ref, *scratch)
+    which = lax.broadcasted_iota(jnp.int32, (2, 128), 0)
+    lane = lax.broadcasted_iota(jnp.int32, (2, 128), 1)
+    ids = jnp.where(which == 0, token_ref[0], token_ref[1])
+    digits = jnp.where(lane == 0, lax.shift_right_logical(ids, 8), jnp.where(lane == 1, ids & 255, 0))
+    digits = digits.astype(F32).astype(BF)
+    out_ref[:, :, cols:] = jnp.broadcast_to(digits[None], (count // 2,) + digits.shape)
+    finish()
+
+
+def second_kernel(low_ref, attr_ref, first_ref, table_ref, out_ref, *scratch):
+    rows, cols = table_ref.shape
+    count = attr_ref.shape[0]
+    low = low_ref[0]
+    extra = first_ref[:, :, cols:].reshape(count, 128).astype(F32)
+    lane = lax.broadcasted_iota(jnp.int32, (count, 128), 1)
+    digits = jnp.where(lane == 0, extra * 256.0, jnp.where(lane == 1, extra, 0.0))
+    ids = jnp.sum(digits, axis=1, keepdims=True)
+    finish = collect(ids, low, table_ref, out_ref, *scratch)
+    mine = 2 * lax.div(low, rows)
+    own = pick(first_ref, [lax.div(attr_ref[mine + i], rows) for i in range(2)], cols)
+    out_ref[:, 2:4, :] = jnp.broadcast_to(own[None], (count // 2, 2, cols))
+    finish()
+
+
+def on_table(kernel, block, low, scalars, values, table):
+    count, cols = 2 * block[0], table.shape[1]
+    table = pltpu.with_memory_space_constraint(table, pltpu.HBM)
     smem = pl.BlockSpec(memory_space=pltpu.SMEM)
     vmem = pl.BlockSpec(memory_space=pltpu.VMEM)
-    table = pltpu.with_memory_space_constraint(table, pltpu.HBM)
-    args = (ids, low, table, extra)
     return pl.pallas_call(
-        functools.partial(gather_kernel, cols),
-        out_shape=jax.ShapeDtypeStruct((count // 2,) + block, BF),
-        in_specs=[smem, smem, pl.BlockSpec(memory_space=pltpu.HBM), vmem],
+        kernel,
+        out_shape=jax.ShapeDtypeStruct(block, BF),
+        in_specs=[smem, smem, vmem, pl.BlockSpec(memory_space=pltpu.HBM)],
         out_specs=vmem,
         scratch_shapes=[
             pltpu.VMEM((count, 8, cols), BF),
-            pltpu.SMEM((count + 1,), jnp.int32),
             pltpu.SemaphoreType.DMA((count,)),
+            pltpu.VMEM((8, count), jnp.int32),
+            pltpu.SemaphoreType.DMA(()),
+            pltpu.SMEM((8, count), jnp.int32),
         ],
         compiler_params=pltpu.CompilerParams(vmem_limit_bytes=16 << 20),
         cost_estimate=pl.CostEstimate(flops=0, transcendentals=0, bytes_accessed=1 << 20),
-    )(*args)
-
-
-def column(row, size):
-    shape = (size, size)
-    same = lax.broadcasted_iota(jnp.int32, shape, 0) == lax.broadcasted_iota(jnp.int32, shape, 1)
-    return jnp.sum(jnp.where(same, row, 0.0), axis=1, keepdims=True)
-
-
-def row_of(col, size):
-    shape = (size, size)
-    same = lax.broadcasted_iota(jnp.int32, shape, 0) == lax.broadcasted_iota(jnp.int32, shape, 1)
-    return jnp.sum(jnp.where(same, col, 0.0), axis=0, keepdims=True)
+    )(low, scalars, values, table)
+
+
+def own_kernel(ids_ref, rows_of_device, blocks_ref, own_ref, out_ref):
+    cols = own_ref.shape[1]
+    own = pick(blocks_ref, [lax.div(ids_ref[i], rows_of_device) for i in range(2)], cols)
+    own_ref[...] = own
+    out_ref[...] = jnp.broadcast_to(own[None], out_ref.shape)
+
+
+def down_kernel(blocks_ref, own_ref, weight_ref, probe_ref, out_ref, logit_ref):
+    probe = blocks_ref[:, 2:4, :].reshape(probe_ref.shape)
+    probe_ref[...] = probe
+    out_ref[...] = contract_last(weight_ref[...], probe).astype(BF)
+    logit_ref[...] = contract_last(own_ref[...], probe)
 
 
 def halves(value):
@@ -100,15 +152,29 @@
     return high, value - high
 
 
-def forward_kernel(rows_ref, gain_ref, weight_ref, own_ref, probe_ref, out_ref):
+def weight_pieces(gate_ref, up_ref, held, sem):
+    hidden = gate_ref.shape[0]
+    main = hidden - 64
+    copy = pltpu.make_async_copy(up_ref, held, sem)
+    copy.start()
+
+    def late():
+        copy.wait()
+        both = jnp.concatenate([gate_ref[main:, :], held[main:, :]], axis=0)
+        return [(main, main + 128, both), (main + 128, 2 * hidden, held[:main, :])]
+
+    return (0, main, gate_ref[:main, :]), late
+
+
+def forward_kernel(rows_ref, gain_ref, own_ref, gate_ref, up_ref, out_ref, held, sem):
+    piece, late = weight_pieces(gate_ref, up_ref, held, sem)
     cols = rows_ref.shape[2]
     tokens = rows_ref.shape[0] * rows_ref.shape[1]
     rows = rows_ref[...].reshape(tokens, cols).astype(F32)
     scaled = (rows * gain_ref[...]).astype(BF)
-    out_ref[0:tokens, :] = contract_last(scaled, weight_ref[...]).astype(BF)
     squares = row_of(jnp.sum(rows * rows, axis=1, keepdims=True), tokens)
     sq_high, sq_low = halves(squares)
-    own_high, own_low = halves(contract_last(own_ref[...], probe_ref[...]))
+    own_high, own_low = halves(own_ref[...])
     at = lax.broadcasted_iota(jnp.int32, (8, tokens), 0)
     side = jnp.zeros((8, tokens), F32)
     lines = [sq_high, sq_low, own_high[0:1], own_high[1:2], own_low[0:1], own_low[1:2]]
@@ -116,6 +182,10 @@
         side = jnp.where(at == i, line, side)
     out_ref[tokens:, 0:tokens] = side.astype(BF)
     out_ref[tokens:, tokens:] = jnp.zeros((8, out_ref.shape[1] - tokens), BF)
+    low, high, weight = piece
+    out_ref[0:tokens, low:high] = contract_last(scaled, weight).astype(BF)
+    for low, high, weight in late():
+        out_ref[0:tokens, low:high] = contract_last(scaled, weight).astype(BF)
 
 
 def middle_kernel(tokens, sums_ref, *rest):
@@ -149,8 +219,9 @@
     )
 
 
-def backward_kernel(grad_ref, down_ref, gate_up_ref, weight_ref, out_ref):
-    cols = weight_ref.shape[1]
+def backward_kernel(grad_ref, down_ref, gate_up_ref, gate_ref, up_ref, out_ref, held, sem):
+    piece, late = weight_pieces(gate_ref, up_ref, held, sem)
+    cols = gate_ref.shape[1]
     gate_up = gate_up_ref[...]
     main = gate_up.shape[1] // 2 - 64
     gate, shared, up = gate_up[:, :main], gate_up[:, main : main + 128], gate_up[:, main + 128 :]
@@ -167,7 +238,10 @@
     lane = lax.broadcasted_iota(jnp.int32, shared.shape, 1)
     tail = jnp.where(lane < 64, tail_gate, pltpu.roll(tail_up, 64, 1))
     grads = jnp.concatenate([gate_grad, tail, up_grad], axis=1).astype(BF)
-    normed = jnp.dot(grads, weight_ref[...], preferred_element_type=F32)
+    low, high, weight = piece
+    normed = jnp.dot(grads[:, low:high], weight, preferred_element_type=F32)
+    for low, high, weight in late():
+        normed = normed + jnp.dot(grads[:, low:high], weight, preferred_element_type=F32)
     shape = out_ref.shape[:2]
     out_ref[:, :, 0:cols] = normed.astype(BF).reshape(shape + (cols,))
     inner = jnp.sum(grads.astype(F32) * gate_up, axis=1, keepdims=True)
@@ -176,13 +250,23 @@
     out_ref[:, :, cols:] = pair.astype(BF).reshape(shape + (128,))
 
 
-def on_core(kernel, out_shape, *args, flops=0):
+def on_core(kernel, out_shape, *args, scalars=(), late=None, flops=0):
+    vmem = pl.BlockSpec(memory_space=pltpu.VMEM)
+    in_specs = [pl.BlockSpec(memory_space=pltpu.SMEM) for _ in scalars] + [vmem for _ in args]
+    scratch = []
+    if late is not None:
+        args = args + (pltpu.with_memory_space_constraint(late, pltpu.HBM),)
+        in_specs.append(pl.BlockSpec(memory_space=pltpu.HBM))
+        scratch = [pltpu.VMEM(late.shape, late.dtype), pltpu.SemaphoreType.DMA(())]
     return pl.pallas_call(
         kernel,
         out_shape=out_shape,
-        compiler_params=pltpu.CompilerParams(vmem_limit_bytes=24 << 20),
+        in_specs=in_specs,
+        out_specs=jax.tree.map(lambda _: vmem, out_shape),
+        scratch_shapes=scratch,
+        compiler_params=pltpu.CompilerParams(vmem_limit_bytes=16 << 20),
         cost_estimate=pl.CostEstimate(flops=flops, transcendentals=0, bytes_accessed=5 << 20),
-    )(*args)
+    )(*scalars, *args)
 
 
 def swap(blocks):
@@ -200,36 +284,43 @@
     ff = w_gate.shape[1]
     logit_scale = 3.0 / math.sqrt(D)
 
-    def pick(received, ids):
-        owner = ids // vocab_rows
-        return jnp.concatenate(
-            [
-                lax.dynamic_slice(received, (owner[i], i, 0), (1, 1, cols)).reshape(1, cols)
-                for i in range(tok_dev)
-            ],
-            axis=0,
+    low = (my_wide * vocab_rows).reshape(1)
+    first = swap(
+        on_table(
+            first_kernel,
+            (wide, tok_dev, cols + 128),
+            low,
+            token_ids,
+            attr_ids.reshape(1, attrs),
+            embed_table,
         )
-
-    main = ff // 128 * 128
-    weight = jnp.concatenate([w_gate.T, w_up.T[main:], w_up.T[:main]], axis=0)
-
-    ids_high = (token_ids // 256).astype(BF)
-    ids_low = (token_ids % 256).astype(BF)
-    extra = jnp.stack([ids_high, ids_low], axis=1)
-    extra = jnp.pad(extra, ((0, 0), (0, 126)))
-    low = (my_wide * vocab_rows).reshape(1)
-    first = swap(gather_rows(attr_ids, low, embed_table, extra))
-    digits = first[:, :, cols : cols + 2].astype(F32)
-    all_ids = (digits[:, :, 0] * 256.0 + digits[:, :, 1]).astype(jnp.int32).reshape(tokens)
-    my_attrs = lax.dynamic_slice_in_dim(attr_ids, my_wide * tok_dev, tok_dev, 0)
-    probe_own, weight = lax.optimization_barrier((pick(first, my_attrs), weight))
-
-    second = swap(gather_rows(all_ids, low, embed_table, probe_own))
-    probe = second[:, tok_dev:, :].reshape(attrs, cols)
-    rows_own = pick(second, token_ids)
-    rows = swap(jnp.broadcast_to(rows_own[None], (wide, tok_dev, cols)))
-
-    down_part = contract_last(w_down, probe).astype(BF)
+    )
+    second = swap(
+        on_table(second_kernel, (wide, 2 * tok_dev, cols), low, attr_ids, first, embed_table)
+    )
+    rows_own, rows = on_core(
+        lambda ids, *refs: own_kernel(ids, vocab_rows, *refs),
+        (
+            jax.ShapeDtypeStruct((tok_dev, cols), BF),
+            jax.ShapeDtypeStruct((wide, tok_dev, cols), BF),
+        ),
+        second,
+        scalars=(token_ids,),
+    )
+    rows = swap(rows)
+
+    probe, down_part, own_part = on_core(
+        down_kernel,
+        (
+            jax.ShapeDtypeStruct((attrs, cols), BF),
+            jax.ShapeDtypeStruct((ff, attrs), BF),
+            jax.ShapeDtypeStruct((tok_dev, attrs), F32),
+        ),
+        second,
+        rows_own,
+        w_down,
+        flops=2 * attrs * cols * ff,
+    )
     down_parts = [down_part]
     for step in range(1, narrow):
         pairs = [(i, (i + step) % narrow) for i in range(narrow)]
@@ -240,9 +331,9 @@
         jax.ShapeDtypeStruct((tokens + 8, 2 * ff), BF),
         rows,
         norm_gain.reshape(1, cols),
-        weight,
-        rows_own,
-        probe,
+        own_part,
+        w_gate.T,
+        late=w_up.T,
         flops=4 * tokens * cols * ff,
     )
     sums = lax.all_gather(part, "narrow", axis=0, tiled=True)
@@ -278,10 +369,11 @@
         logit_grad,
         down_probe,
         gate_up,
-        weight,
+        w_gate.T,
+        late=w_up.T,
         flops=4 * tokens * cols * ff,
     )
-    last = swap(last)
+    last, out_grad = lax.optimization_barrier((swap(last), out_grad))
     last = jnp.sum(last.astype(F32), axis=0)
     scaled = last[:, :cols] * norm_gain
     inner = last[:, cols : cols + 1] + last[:, cols + 1 : cols + 2]

time: 161 us -> 152 us (0.944)
  blocking collectives: 34 us -> 81.3 us
  starting transfers between devices: 47 us -> 27.8 us
  waiting for transfers between devices: 36.6 us -> 20.7 us
  local copies, waits for them, and re-layouts: 14.3 us -> 4.44 us
  between operations: 7.58 us -> 0.2 us
  other arithmetic: 7.45 us -> 1.81 us
  Pallas kernels: 11.8 us -> 14.6 us
    all_to_all x1 -> x3, blocking collectives: 11.9 us -> 57.4 us  [swap(): return lax.all_to_all(blocks, 'wide', 0, 0, tiled=True)]
    all_to_all x5 -> x3, starting transfers between devices: 37.3 us -> 18.3 us  [swap(): return lax.all_to_all(blocks, 'wide', 0, 0, tiled=True)]
    all_to_all x5 -> x3, waiting for transfers between devices: 36.6 us -> 20.7 us  [swap(): return lax.all_to_all(blocks, 'wide', 0, 0, tiled=True)]
    slice x5 -> x0, local copies, waits for them, and re-layouts: 6.17 us -> none  [the longest x2 3.19 us: body(): weight = jnp.concatenate([w_gate.T, w_up.T[main:], w_up.T[:main]], axis=0)]
    concatenate x3 -> x0, other arithmetic: 3.34 us -> none  [the longest x1 3.29 us: body(): weight = jnp.concatenate([w_gate.T, w_up.T[main:], w_up.T[:main]], axis=0)]
    pallas_call x5 -> x7, Pallas kernels: 11.8 us -> 14.6 us  [the longest x5 8.02 us: on_core(): pl.pallas_call(kernel, out_shape=out_shape, in_specs=in_specs, out_specs=...]
    all_gather x1, blocking collectives: 22 us -> 23.9 us  [body(): sums = lax.all_gather(part, 'narrow', axis=0, tiled=True)]
    unnamed x18 -> x24, local copies, waits for them, and re-layouts: 5.74 us -> 4.41 us
  transfers between devices with their start and end apart: 8 -> 6, of which waited for: 5 -> 2; matrix products, arithmetic and copies ran while one was open for 6% -> 0% of each run, Pallas kernels for 1% -> 2%
where the time goes in v3:
time: 152 us; the launch traced here: 151 us
  blocking collectives  81.3 us (53%)
  starting transfers between devices  27.8 us (18%)
  waiting for transfers between devices  20.7 us (14%)
  Pallas kernels  14.6 us (10%)
  local copies, waits for them, and re-layouts  4.44 us (3%)
  other arithmetic  1.81 us (1%)
    all_to_all x3, blocking collectives, swap(): return lax.all_to_all(blocks, 'wide', 0, 0, tiled=True)  57.4 us
    all_gather x1, blocking collectives, body(): sums = lax.all_gather(part, 'narrow', axis=0, tiled=True)  23.9 us
    all_to_all x3, waiting for transfers between devices, swap(): return lax.all_to_all(blocks, 'wide', 0, 0, tiled=True)  20.7 us
    all_to_all x3, starting transfers between devices, swap(): return lax.all_to_all(blocks, 'wide', 0, 0, tiled=True)  18.3 us
    ppermute x3, starting transfers between devices, body(): down_parts.append(lax.ppermute(down_part, 'narrow', pairs))  9.58 us
    pallas_call x5, Pallas kernels, on_core(): pl.pallas_call(kernel, out_shape=out_shape, in_specs=in_specs, out_specs=...  8.02 us
    pallas_call x2, Pallas kernels, on_table(): pl.pallas_call(kernel, out_shape=jax.ShapeDtypeStruct(block, BF), in_spec...  6.63 us
    unnamed x24, local copies, waits for them, and re-layouts  4.41 us
  transfers between devices with their start and end apart: 6, of which 2 were waited for; matrix products, arithmetic and copies ran while one was open for 0% of the time, Pallas kernels for 2%

profile of v3, /device:TPU:1, one launch (start us, length us, event | category | flops | bytes accessed | tf_op | source)
XLA Modules:
  0.0 151.1 jit_solution(9884780854344401791)
XLA Ops:
  0.0 0.7 copy-done.6
  0.7 0.7 copy-done.8
  1.3 3.3 %shard_map.91 = bf16[64,2,2176]{2,1,0:T(2,128)(2,1)S(1)} custom-call(s32[1]{0:T(128)} %bitcast.low_ref, s32[2]{0:T(128)S(1)} %copy-done.8, s32[1,128]{1,0:T(1,128)S(1)} %bitcast.13, bf16[1024,2048]{1,0:T(8,128)(2,1)} %table_ref.3), custom_call_target="tpu_custom_call" | custom-call | bytes 1048576 | tf_op jit(solution)/shard_map/pallas_call | solution.py:119
  4.6 23.0 %all_to_all.30.first_ref = bf16[64,2,2176]{2,1,0:T(2,128)(2,1)S(1)} all-to-all(bf16[64,2,2176]{2,1,0:T(2,128)(2,1)S(1)} %shard_map.91), channel_id=1, replica_groups=mesh['wide'=64,'narrow'=4] {'wide'}, dimensions={0} | all-to-all | bytes 1114112 | tf_op jit(solution)/shard_map/all_to_all | solution.py:273
  27.6 3.3 %shard_map.92 = bf16[64,4,2048]{2,1,0:T(4,128)(2,1)S(1)} custom-call(s32[1]{0:T(128)} %bitcast.low_ref, s32[128]{0:T(128)S(1)} %copy-done.7, bf16[64,2,2176]{2,1,0:T(2,128)(2,1)S(1)} %all_to_all.30.first_ref, bf16[1024,2048]{1,0:T(8,128)(2,1)} %table_ref.3), custom_call_target="tpu_custom_call" | custom-call | bytes 1048576 | tf_op jit(solution)/shard_map/pallas_call | solution.py:119
  31.0 22.4 %all_to_all.31.refs_0_.blocks_ref = bf16[64,4,2048]{2,1,0:T(4,128)(2,1)S(1)} all-to-all(bf16[64,4,2048]{2,1,0:T(4,128)(2,1)S(1)} %shard_map.92), channel_id=1, replica_groups=mesh['wide'=64,'narrow'=4] {'wide'}, dimensions={0} | all-to-all | bytes 2097152 | tf_op jit(solution)/shard_map/all_to_all | solution.py:273
  54.0 0.8 copy-done.4
  54.8 4.8 %all-to-all-start.2 = ((bf16[64,2,2048]{2,1,0:T(2,128)(2,1)}), bf16[64,2,2048]{2,1,0:T(2,128)(2,1)S(1)}, u32[]{:S(2)}, u32[]{:S(2)}) async-start(bf16[64,2,2048]{2,1,0:T(2,128)(2,1)} %copy-done.4), calls=%async_computation.2 | async-start | bytes 1048576 | tf_op jit(solution)/shard_map/all_to_all | solution.py:273
  59.6 1.5 copy-done.1
  61.1 0.8 shard_map.94
  62.0 0.8 copy-done.2
  62.7 3.0 %collective-permute-start = (bf16[448,128]{1,0:T(8,128)(2,1)S(1)}, bf16[448,128]{1,0:T(8,128)(2,1)S(1)}, u32[]{:S(2)}, u32[]{:S(2)}) collective-permute-start(bf16[448,128]{1,0:T(8,128)(2,1)S(1)} %get-tuple-element.20.rest_0_), channel_id=1, source_target_pairs={{0,1},{1,2},{2,3},{3,0},{4,5},{5,6},{6,7},{7,4},{8,9},{9,10},{10,1... | collective-permute-start | bytes 344072 | tf_op jit(solution)/shard_map/ppermute | solution.py:327
  65.7 4.2 %collective-permute-start.1 = (bf16[448,128]{1,0:T(8,128)(2,1)S(1)}, bf16[448,128]{1,0:T(8,128)(2,1)S(1)}, u32[]{:S(2)}, u32[]{:S(2)}) collective-permute-start(bf16[448,128]{1,0:T(8,128)(2,1)S(1)} %get-tuple-element.20.rest_0_), channel_id=1, source_target_pairs={{0,2},{1,3},{2,0},{3,1},{4,6},{5,7},{6,4},{7,5},{8,10},{9,11},{10,... | collective-permute-start | bytes 344072 | tf_op jit(solution)/shard_map/ppermute | solution.py:327
  69.9 2.4 %collective-permute-start.2 = (bf16[448,128]{1,0:T(8,128)(2,1)S(1)}, bf16[448,128]{1,0:T(8,128)(2,1)S(1)}, u32[]{:S(2)}, u32[]{:S(2)}) collective-permute-start(bf16[448,128]{1,0:T(8,128)(2,1)S(1)} %get-tuple-element.20.rest_0_), channel_id=1, source_target_pairs={{0,3},{1,0},{2,1},{3,2},{4,7},{5,4},{6,5},{7,6},{8,11},{9,8},{10,9... | collective-permute-start | bytes 344072 | tf_op jit(solution)/shard_map/ppermute | solution.py:327
  72.3 2.2 %shard_map.95 = bf16[136,896]{1,0:T(8,128)(2,1)S(1)} custom-call(bf16[64,2,2048]{2,1,0:T(2,128)(2,1)S(1)} %all-to-all-done.2.rows_ref, f32[1,2048]{1,0:T(1,128)S(1)} %bitcast.12, f32[2,128]{1,0:T(2,128)S(1)} %get-tuple-element.19.own_ref, bf16[448,2048]{1,0:T(8,128)(2,1)S(1)} %bitcast.9, bf16[448,2048]{1,0:T(8,128)(2,1)} %bitcast.14), custom_call_target="tpu_custom_call" | custom-call | flops 469762048 | bytes 5242880 | tf_op jit(solution)/shard_map/pallas_call | solution.py:261
  74.6 23.9 %all_gather.3.sums_ref = bf16[544,896]{1,0:T(8,128)(2,1)S(1)} all-gather(bf16[136,896]{1,0:T(8,128)(2,1)S(1)} %shard_map.95), channel_id=1, replica_groups=mesh['wide'=64,'narrow'=4] {'narrow'}, dimensions={0}, use_global_device_ids=true | all-gather | bytes 1218560 | tf_op jit(solution)/shard_map/all_gather | solution.py:339
  98.5 1.0 shard_map.96
  99.6 8.7 %all-to-all-start.3 = ((f32[64,2,128]{2,1,0:T(2,128)}), f32[64,2,128]{2,1,0:T(2,128)S(1)}, u32[]{:S(2)}, u32[]{:S(2)}) async-start(f32[64,2,128]{2,1,0:T(2,128)} %bitcast.5), calls=%async_computation.3 | async-start | bytes 131072 | tf_op jit(solution)/shard_map/all_to_all | solution.py:273
  108.3 8.1 %all-to-all-done.3 = f32[64,2,128]{2,1,0:T(2,128)S(1)} async-done(((f32[64,2,128]{2,1,0:T(2,128)}), f32[64,2,128]{2,1,0:T(2,128)S(1)}, u32[]{:S(2)}, u32[]{:S(2)}) %all-to-all-start.3) | async-done | bytes 65568 | tf_op jit(solution)/shard_map/all_to_all | solution.py:273
  116.9 11.9 %all_to_all.32 = bf16[64,2,128]{2,1,0:T(2,128)(2,1)S(1)} all-to-all(bf16[64,2,128]{2,1,0:T(2,128)(2,1)S(1)} %broadcast_in_dim.2), channel_id=1, replica_groups=mesh['wide'=64,'narrow'=4] {'wide'}, dimensions={0} | all-to-all | bytes 65536 | tf_op jit(solution)/shard_map/all_to_all | solution.py:273
  128.8 3.3 %shard_map.97 = bf16[64,2,2176]{2,1,0:T(2,128)(2,1)} custom-call(bf16[128,128]{1,0:T(8,128)(2,1)S(1)} %bitcast.11, bf16[448,128]{1,0:T(8,128)(2,1)S(1)} %get-tuple-element.23.down_ref, f32[128,896]{1,0:T(8,128)S(1)} %get-tuple-element.24.gate_up_ref, bf16[448,2048]{1,0:T(8,128)(2,1)S(1)} %bitcast.10, bf16[448,2048]{1,0:T(8,128)(2,1)} %bitcast.15), custom_call_target="tpu_custom_call" | custom-call | flops 469762048 | bytes 5242880 | tf_op jit(solution)/shard_map/pallas_call | solution.py:261
  132.2 4.7 %all-to-all-start.5 = ((bf16[64,2,2176]{2,1,0:T(2,128)(2,1)}), bf16[64,2,2176]{2,1,0:T(2,128)(2,1)S(1)}, u32[]{:S(2)}, u32[]{:S(2)}) async-start(bf16[64,2,2176]{2,1,0:T(2,128)(2,1)} %shard_map.97), calls=%async_computation.5 | async-start | bytes 1114112 | tf_op jit(solution)/shard_map/all_to_all | solution.py:273
  137.1 12.7 %all-to-all-done.5 = bf16[64,2,2176]{2,1,0:T(2,128)(2,1)S(1)} async-done(((bf16[64,2,2176]{2,1,0:T(2,128)(2,1)}), bf16[64,2,2176]{2,1,0:T(2,128)(2,1)S(1)}, u32[]{:S(2)}, u32[]{:S(2)}) %all-to-all-start.5) | async-done | bytes 557088 | tf_op jit(solution)/shard_map/all_to_all | solution.py:273
  150.4 0.7 fusion.3
  (34 shorter events, 2.0 us)
Async XLA Ops:
  0.0 0.7 copy-start.6
  0.7 0.7 copy-start.8
  1.3 26.3 %copy-start.7 = (s32[128]{0:T(128)S(1)}, s32[128]{0:T(128)}, u32[]{:S(2)}) copy-start(s32[128]{0:T(128)} %attr_ref.1) | copy-start | bytes 1540
  31.0 22.4 %copy-start.9 = (s32[2]{0:T(128)S(1)}, s32[2]{0:T(128)}, u32[]{:S(2)}) copy-start(s32[2]{0:T(128)} %ids.1) | copy-start | bytes 28
  54.0 0.8 copy-start.4
  54.8 17.5 %copy-start = (bf16[2048,448]{0,1:T(8,128)(2,1)S(1)}, bf16[2048,448]{0,1:T(8,128)(2,1)}, u32[]{:S(2)}) copy-start(bf16[2048,448]{0,1:T(8,128)(2,1)} %param.15) | copy-start | bytes 5505028
  54.8 17.5 %all-to-all-start.2 = ((bf16[64,2,2048]{2,1,0:T(2,128)(2,1)}), bf16[64,2,2048]{2,1,0:T(2,128)(2,1)S(1)}, u32[]{:S(2)}, u32[]{:S(2)}) async-start(bf16[64,2,2048]{2,1,0:T(2,128)(2,1)} %copy-done.4), calls=%async_computation.2 | async-start | bytes 1048576 | tf_op jit(solution)/shard_map/all_to_all | solution.py:273
  59.6 1.5 copy-start.1
  61.1 11.2 %copy-start.5 = (f32[2048]{0:T(1024)S(1)}, f32[2048]{0:T(1024)}, u32[]{:S(2)}) copy-start(f32[2048]{0:T(1024)} %param.14) | copy-start | bytes 24580
  61.9 0.8 copy-start.2
  62.7 35.8 %collective-permute-start = (bf16[448,128]{1,0:T(8,128)(2,1)S(1)}, bf16[448,128]{1,0:T(8,128)(2,1)S(1)}, u32[]{:S(2)}, u32[]{:S(2)}) collective-permute-start(bf16[448,128]{1,0:T(8,128)(2,1)S(1)} %get-tuple-element.20.rest_0_), channel_id=1, source_target_pairs={{0,1},{1,2},{2,3},{3,0},{4,5},{5,6},{6,7},{7,4},{8,9},{9,10},{10,1... | collective-permute-start | bytes 344072 | tf_op jit(solution)/shard_map/ppermute | solution.py:327
  65.7 32.8 %collective-permute-start.1 = (bf16[448,128]{1,0:T(8,128)(2,1)S(1)}, bf16[448,128]{1,0:T(8,128)(2,1)S(1)}, u32[]{:S(2)}, u32[]{:S(2)}) collective-permute-start(bf16[448,128]{1,0:T(8,128)(2,1)S(1)} %get-tuple-element.20.rest_0_), channel_id=1, source_target_pairs={{0,2},{1,3},{2,0},{3,1},{4,6},{5,7},{6,4},{7,5},{8,10},{9,11},{10,... | collective-permute-start | bytes 344072 | tf_op jit(solution)/shard_map/ppermute | solution.py:327
  69.9 28.6 %collective-permute-start.2 = (bf16[448,128]{1,0:T(8,128)(2,1)S(1)}, bf16[448,128]{1,0:T(8,128)(2,1)S(1)}, u32[]{:S(2)}, u32[]{:S(2)}) collective-permute-start(bf16[448,128]{1,0:T(8,128)(2,1)S(1)} %get-tuple-element.20.rest_0_), channel_id=1, source_target_pairs={{0,3},{1,0},{2,1},{3,2},{4,7},{5,4},{6,5},{7,6},{8,11},{9,8},{10,9... | collective-permute-start | bytes 344072 | tf_op jit(solution)/shard_map/ppermute | solution.py:327
  74.6 33.7 %copy-start.11 = (s32[2]{0:T(128)S(1)}, s32[2]{0:T(128)}, u32[]{:S(2)}) copy-start(s32[2]{0:T(128)} %param.12) | copy-start | bytes 28
  74.6 42.2 %copy-start.10 = (s32[2]{0:T(128)S(1)}, s32[2]{0:T(128)}, u32[]{:S(2)}) copy-start(s32[2]{0:T(128)} %param.11) | copy-start | bytes 28
  99.6 16.8 %all-to-all-start.3 = ((f32[64,2,128]{2,1,0:T(2,128)}), f32[64,2,128]{2,1,0:T(2,128)S(1)}, u32[]{:S(2)}, u32[]{:S(2)}) async-start(f32[64,2,128]{2,1,0:T(2,128)} %bitcast.5), calls=%async_computation.3 | async-start | bytes 131072 | tf_op jit(solution)/shard_map/all_to_all | solution.py:273
  128.8 8.1 %copy-start.3 = (bf16[128,2048]{1,0:T(8,128)(2,1)S(1)}, bf16[128,2048]{1,0:T(8,128)(2,1)}, u32[]{:S(2)}) copy-start(bf16[128,2048]{1,0:T(8,128)(2,1)} %copy-done.2) | copy-start | bytes 1572868
  132.2 17.6 %all-to-all-start.5 = ((bf16[64,2,2176]{2,1,0:T(2,128)(2,1)}), bf16[64,2,2176]{2,1,0:T(2,128)(2,1)S(1)}, u32[]{:S(2)}, u32[]{:S(2)}) async-start(bf16[64,2,2176]{2,1,0:T(2,128)(2,1)} %shard_map.97), calls=%async_computation.5 | async-start | bytes 1114112 | tf_op jit(solution)/shard_map/all_to_all | solution.py:273

commit v4 on v3

--- a/solution.py
+++ b/solution.py
@@ -76,17 +76,52 @@
     return lambda: lax.fori_loop(0, list_ref[2, 0], put, 0)
 
 
+def collect_listed(ids, low, table_ref, out_ref, held, found, sems, count):
+    rows, cols = table_ref.shape
+    total = jnp.int32(0)
+    for i in range(count):
+        local = ids(i) - low
+        found[total] = i
+        total = total + ((local >= 0) & (local < rows)).astype(jnp.int32)
+
+    def copy(k):
+        local = jnp.clip(ids(found[k]) - low, 0, rows - 1)
+        start = pl.multiple_of(lax.shift_left(lax.shift_right_logical(local, 3), 3), 8)
+        return pltpu.make_async_copy(table_ref.at[pl.ds(start, 8), :], held.at[k], sems.at[k])
+
+    def begin(k, carry):
+        copy(k).start()
+        return carry
+
+    lax.fori_loop(0, total, begin, 0)
+
+    def place(k, carry):
+        copy(k).wait()
+        i = found[k]
+        row = lax.broadcasted_iota(jnp.int32, (8, cols), 0)
+        wanted = jnp.where(row == ((ids(i) - low) & 7), held[k].astype(F32), 0.0)
+        wanted = jnp.sum(wanted, axis=0, keepdims=True)
+        which = lax.broadcasted_iota(jnp.int32, (2, cols), 0)
+        pair = lax.shift_right_logical(i, 1)
+        before = out_ref[pair, 0:2, 0:cols].astype(F32)
+        out_ref[pair, 0:2, 0:cols] = jnp.where(which == (i & 1), wanted, before).astype(BF)
+        return carry
+
+    return lambda: lax.fori_loop(0, total, place, 0)
+
+
 def pick(blocks_ref, ids, cols):
     which = lax.broadcasted_iota(jnp.int32, (2, cols), 0)
     blocks = [blocks_ref[owner, 0:2, 0:cols].astype(F32) for owner in ids]
     return jnp.where(which == 0, blocks[0], blocks[1]).astype(BF)
 
 
-def first_kernel(low_ref, token_ref, ids_ref, table_ref, out_ref, *scratch):
+def first_kernel(low_ref, token_ref, ids_ref, table_ref, out_ref, held, sems, *found):
     cols = table_ref.shape[1]
-    count = ids_ref.shape[1]
-    ids = column(ids_ref[...].astype(F32), count)
-    finish = collect(ids, low_ref[0], table_ref, out_ref, *scratch)
+    count = ids_ref.shape[0]
+    finish = collect_listed(
+        lambda i: ids_ref[i], low_ref[0], table_ref, out_ref, held, found[0], sems, count
+    )
     which = lax.broadcasted_iota(jnp.int32, (2, 128), 0)
     lane = lax.broadcasted_iota(jnp.int32, (2, 128), 1)
     ids = jnp.where(which == 0, token_ref[0], token_ref[1])
@@ -119,14 +154,25 @@
     return pl.pallas_call(
         kernel,
         out_shape=jax.ShapeDtypeStruct(block, BF),
-        in_specs=[smem, smem, vmem, pl.BlockSpec(memory_space=pltpu.HBM)],
+        in_specs=[
+            smem,
+            smem,
+            smem if values.ndim == 1 else vmem,
+            pl.BlockSpec(memory_space=pltpu.HBM),
+        ],
         out_specs=vmem,
         scratch_shapes=[
             pltpu.VMEM((count, 8, cols), BF),
             pltpu.SemaphoreType.DMA((count,)),
-            pltpu.VMEM((8, count), jnp.int32),
-            pltpu.SemaphoreType.DMA(()),
-            pltpu.SMEM((8, count), jnp.int32),
+            *(
+                [pltpu.SMEM((count + 1,), jnp.int32)]
+                if values.ndim == 1
+                else [
+                    pltpu.VMEM((8, count), jnp.int32),
+                    pltpu.SemaphoreType.DMA(()),
+                    pltpu.SMEM((8, count), jnp.int32),
+                ]
+            ),
         ],
         compiler_params=pltpu.CompilerParams(vmem_limit_bytes=16 << 20),
         cost_estimate=pl.CostEstimate(flops=0, transcendentals=0, bytes_accessed=1 << 20),
@@ -219,7 +265,9 @@
     )
 
 
-def backward_kernel(grad_ref, down_ref, gate_up_ref, gate_ref, up_ref, out_ref, held, sem):
+def backward_kernel(
+    core_ref, grad_ref, down_ref, gate_up_ref, gate_ref, up_ref, mine_ref, other_ref, held, sem
+):
     piece, late = weight_pieces(gate_ref, up_ref, held, sem)
     cols = gate_ref.shape[1]
     gate_up = gate_up_ref[...]
@@ -242,12 +290,17 @@
     normed = jnp.dot(grads[:, low:high], weight, preferred_element_type=F32)
     for low, high, weight in late():
         normed = normed + jnp.dot(grads[:, low:high], weight, preferred_element_type=F32)
-    shape = out_ref.shape[:2]
-    out_ref[:, :, 0:cols] = normed.astype(BF).reshape(shape + (cols,))
     inner = jnp.sum(grads.astype(F32) * gate_up, axis=1, keepdims=True)
     high, low = halves(inner)
     pair = jnp.where(lane == 0, high, jnp.where(lane == 1, low, 0.0))
-    out_ref[:, :, cols:] = pair.astype(BF).reshape(shape + (128,))
+    chips = mine_ref.shape[0]
+    first = core_ref[0] == 0
+    for start, value in ((0, normed), (cols, pair)):
+        width = value.shape[1]
+        value = value.astype(BF).reshape(chips, 2, 2, width)
+        even, odd = value[:, 0].astype(F32), value[:, 1].astype(F32)
+        mine_ref[:, :, start : start + width] = jnp.where(first, even, odd).astype(BF)
+        other_ref[:, :, start : start + width] = jnp.where(first, odd, even).astype(BF)
 
 
 def on_core(kernel, out_shape, *args, scalars=(), late=None, flops=0):
@@ -291,7 +344,7 @@
             (wide, tok_dev, cols + 128),
             low,
             token_ids,
-            attr_ids.reshape(1, attrs),
+            attr_ids,
             embed_table,
         )
     )
@@ -363,17 +416,23 @@
     )
     out_grad = jnp.dot(grad_own, probe, preferred_element_type=F32)
 
-    last = on_core(
+    half = jax.ShapeDtypeStruct((wide // 2, tok_dev, cols + 128), BF)
+    mine, other = on_core(
         backward_kernel,
-        jax.ShapeDtypeStruct((wide, tok_dev, cols + 128), BF),
+        (half, half),
         logit_grad,
         down_probe,
         gate_up,
         w_gate.T,
         late=w_up.T,
+        scalars=((my_wide % 2).reshape(1),),
         flops=4 * tokens * cols * ff,
     )
-    last, out_grad = lax.optimization_barrier((swap(last), out_grad))
+    got = lax.ppermute(other, "wide", [(i, i ^ 1) for i in range(wide)])
+    last = (mine.astype(F32) + got.astype(F32)).astype(BF)
+    cores = [list(range(core, wide, 2)) for core in range(2)]
+    last = lax.all_to_all(last, "wide", 0, 0, tiled=True, axis_index_groups=cores)
+    last, out_grad = lax.optimization_barrier((last, out_grad))
     last = jnp.sum(last.astype(F32), axis=0)
     scaled = last[:, :cols] * norm_gain
     inner = last[:, cols : cols + 1] + last[:, cols + 1 : cols + 2]

time: 152 us -> 149 us (0.980)
  blocking collectives: 81.3 us -> 68.7 us
  starting transfers between devices: 27.8 us -> 32.6 us
  waiting for transfers between devices: 20.7 us -> 25.2 us
    all_to_all x3 -> x2, blocking collectives: 57.4 us -> 45.3 us  [swap(): return lax.all_to_all(blocks, 'wide', 0, 0, tiled=True)]
    all_to_all x0 -> x1, waiting for transfers between devices: none -> 8.03 us  [body(): lax.all_to_all(last, 'wide', 0, 0, tiled=True, axis_index_groups=cores)]
    all_to_all x3, waiting for transfers between devices: 20.7 us -> 15.9 us  [swap(): return lax.all_to_all(blocks, 'wide', 0, 0, tiled=True)]
    all_to_all x0 -> x1, starting transfers between devices: none -> 3.87 us  [body(): lax.all_to_all(last, 'wide', 0, 0, tiled=True, axis_index_groups=cores)]
  transfers between devices with their start and end apart: 6 -> 8, of which waited for: 2 -> 4; matrix products, arithmetic and copies ran while one was open for 0% -> 0% of each run, Pallas kernels for 2% -> 2%
where the time goes in v4:
time: 149 us; the launch traced here: 148 us
  blocking collectives  68.7 us (46%)
  starting transfers between devices  32.6 us (22%)
  waiting for transfers between devices  25.2 us (17%)
  Pallas kernels  13.8 us (9%)
  local copies, waits for them, and re-layouts  5.08 us (3%)
  other arithmetic  2.57 us (2%)
    all_to_all x2, blocking collectives, swap(): return lax.all_to_all(blocks, 'wide', 0, 0, tiled=True)  45.3 us
    all_gather x1, blocking collectives, body(): sums = lax.all_gather(part, 'narrow', axis=0, tiled=True)  23.3 us
    all_to_all x3, starting transfers between devices, swap(): return lax.all_to_all(blocks, 'wide', 0, 0, tiled=True)  18.4 us
    all_to_all x3, waiting for transfers between devices, swap(): return lax.all_to_all(blocks, 'wide', 0, 0, tiled=True)  15.9 us
    ppermute x3, starting transfers between devices, body(): down_parts.append(lax.ppermute(down_part, 'narrow', pairs))  9.59 us
    all_to_all x1, waiting for transfers between devices, body(): lax.all_to_all(last, 'wide', 0, 0, tiled=True, axis_index_groups=cores)  8.03 us
    pallas_call x5, Pallas kernels, on_core(): pl.pallas_call(kernel, out_shape=out_shape, in_specs=in_specs, out_specs=...  7.56 us
    pallas_call x2, Pallas kernels, on_table(): pl.pallas_call(kernel, out_shape=jax.ShapeDtypeStruct(block, BF), in_spec...  6.26 us
  transfers between devices with their start and end apart: 8, of which 4 were waited for; matrix products, arithmetic and copies ran while one was open for 0% of the time, Pallas kernels for 2%

profile of v4, /device:TPU:1, one launch (start us, length us, event | category | flops | bytes accessed | tf_op | source)
XLA Modules:
  0.0 148.3 jit_solution(10370706425871870461)
XLA Ops:
  1.3 2.9 %shard_map.91 = bf16[64,2,2176]{2,1,0:T(2,128)(2,1)S(1)} custom-call(s32[1]{0:T(128)} %bitcast.1.low_ref, s32[2]{0:T(128)S(1)} %copy-done.8, s32[128]{0:T(128)S(1)} %copy-done.6, bf16[1024,2048]{1,0:T(8,128)(2,1)} %table_ref.3), custom_call_target="tpu_custom_call" | custom-call | bytes 1048576 | tf_op jit(solution)/shard_map/pallas_call | solution.py:154
  4.3 22.9 %all_to_all.30.first_ref = bf16[64,2,2176]{2,1,0:T(2,128)(2,1)S(1)} all-to-all(bf16[64,2,2176]{2,1,0:T(2,128)(2,1)S(1)} %shard_map.91), channel_id=1, replica_groups=mesh['wide'=64,'narrow'=4] {'wide'}, dimensions={0} | all-to-all | bytes 1114112 | tf_op jit(solution)/shard_map/all_to_all | solution.py:326
  27.1 3.3 %shard_map.92 = bf16[64,4,2048]{2,1,0:T(4,128)(2,1)S(1)} custom-call(s32[1]{0:T(128)} %bitcast.1.low_ref, s32[128]{0:T(128)S(1)} %copy-done.7, bf16[64,2,2176]{2,1,0:T(2,128)(2,1)S(1)} %all_to_all.30.first_ref, bf16[1024,2048]{1,0:T(8,128)(2,1)} %table_ref.3), custom_call_target="tpu_custom_call" | custom-call | bytes 1048576 | tf_op jit(solution)/shard_map/pallas_call | solution.py:154
  30.5 22.4 %all_to_all.31.refs_0_.blocks_ref = bf16[64,4,2048]{2,1,0:T(4,128)(2,1)S(1)} all-to-all(bf16[64,4,2048]{2,1,0:T(4,128)(2,1)S(1)} %shard_map.92), channel_id=1, replica_groups=mesh['wide'=64,'narrow'=4] {'wide'}, dimensions={0} | all-to-all | bytes 2097152 | tf_op jit(solution)/shard_map/all_to_all | solution.py:326
  53.5 0.8 copy-done.4
  54.3 4.8 %all-to-all-start.2 = ((bf16[64,2,2048]{2,1,0:T(2,128)(2,1)}), bf16[64,2,2048]{2,1,0:T(2,128)(2,1)S(1)}, u32[]{:S(2)}, u32[]{:S(2)}) async-start(bf16[64,2,2048]{2,1,0:T(2,128)(2,1)} %copy-done.4), calls=%async_computation.2 | async-start | bytes 1048576 | tf_op jit(solution)/shard_map/all_to_all | solution.py:326
  59.1 1.5 %copy-done.1 = bf16[448,2048]{1,0:T(8,128)(2,1)S(1)} copy-done((bf16[448,2048]{1,0:T(8,128)(2,1)S(1)}, bf16[448,2048]{1,0:T(8,128)(2,1)}, u32[]{:S(2)}) %copy-start.1) | copy-done | bytes 1835032
  60.6 0.8 shard_map.94
  61.5 0.8 copy-done.2
  62.3 3.0 %collective-permute-start = (bf16[448,128]{1,0:T(8,128)(2,1)S(1)}, bf16[448,128]{1,0:T(8,128)(2,1)S(1)}, u32[]{:S(2)}, u32[]{:S(2)}) collective-permute-start(bf16[448,128]{1,0:T(8,128)(2,1)S(1)} %get-tuple-element.22.rest_0_), channel_id=1, source_target_pairs={{0,1},{1,2},{2,3},{3,0},{4,5},{5,6},{6,7},{7,4},{8,9},{9,10},{10,1... | collective-permute-start | bytes 344072 | tf_op jit(solution)/shard_map/ppermute | solution.py:380
  65.3 4.2 %collective-permute-start.1 = (bf16[448,128]{1,0:T(8,128)(2,1)S(1)}, bf16[448,128]{1,0:T(8,128)(2,1)S(1)}, u32[]{:S(2)}, u32[]{:S(2)}) collective-permute-start(bf16[448,128]{1,0:T(8,128)(2,1)S(1)} %get-tuple-element.22.rest_0_), channel_id=1, source_target_pairs={{0,2},{1,3},{2,0},{3,1},{4,6},{5,7},{6,4},{7,5},{8,10},{9,11},{10,... | collective-permute-start | bytes 344072 | tf_op jit(solution)/shard_map/ppermute | solution.py:380
  69.5 2.4 %collective-permute-start.2 = (bf16[448,128]{1,0:T(8,128)(2,1)S(1)}, bf16[448,128]{1,0:T(8,128)(2,1)S(1)}, u32[]{:S(2)}, u32[]{:S(2)}) collective-permute-start(bf16[448,128]{1,0:T(8,128)(2,1)S(1)} %get-tuple-element.22.rest_0_), channel_id=1, source_target_pairs={{0,3},{1,0},{2,1},{3,2},{4,7},{5,4},{6,5},{7,6},{8,11},{9,8},{10,9... | collective-permute-start | bytes 344072 | tf_op jit(solution)/shard_map/ppermute | solution.py:380
  71.9 2.2 %shard_map.95 = bf16[136,896]{1,0:T(8,128)(2,1)S(1)} custom-call(bf16[64,2,2048]{2,1,0:T(2,128)(2,1)S(1)} %all-to-all-done.2.rows_ref, f32[1,2048]{1,0:T(1,128)S(1)} %bitcast.12, f32[2,128]{1,0:T(2,128)S(1)} %get-tuple-element.21.own_ref, bf16[448,2048]{1,0:T(8,128)(2,1)S(1)} %bitcast.9, bf16[448,2048]{1,0:T(8,128)(2,1)} %bitcast.13), custom_call_target="tpu_custom_call" | custom-call | flops 469762048 | bytes 5242880 | tf_op jit(solution)/shard_map/pallas_call | solution.py:314
  74.1 23.3 %all_gather.3.sums_ref = bf16[544,896]{1,0:T(8,128)(2,1)S(1)} all-gather(bf16[136,896]{1,0:T(8,128)(2,1)S(1)} %shard_map.95), channel_id=1, replica_groups=mesh['wide'=64,'narrow'=4] {'narrow'}, dimensions={0}, use_global_device_ids=true | all-gather | bytes 1218560 | tf_op jit(solution)/shard_map/all_gather | solution.py:392
  97.5 1.0 shard_map.96
  98.5 9.2 %all-to-all-start.3 = ((f32[64,2,128]{2,1,0:T(2,128)}), f32[64,2,128]{2,1,0:T(2,128)S(1)}, u32[]{:S(2)}, u32[]{:S(2)}) async-start(f32[64,2,128]{2,1,0:T(2,128)} %bitcast.5), calls=%async_computation.3 | async-start | bytes 131072 | tf_op jit(solution)/shard_map/all_to_all | solution.py:326
  107.8 8.1 %all-to-all-done.3 = f32[64,2,128]{2,1,0:T(2,128)S(1)} async-done(((f32[64,2,128]{2,1,0:T(2,128)}), f32[64,2,128]{2,1,0:T(2,128)S(1)}, u32[]{:S(2)}, u32[]{:S(2)}) %all-to-all-start.3) | async-done | bytes 65568 | tf_op jit(solution)/shard_map/all_to_all | solution.py:326
  117.0 4.4 %all-to-all-start.4 = ((bf16[64,2,128]{2,1,0:T(2,128)(2,1)}), bf16[64,2,128]{2,1,0:T(2,128)(2,1)S(1)}, u32[]{:S(2)}, u32[]{:S(2)}) async-start(bf16[64,2,128]{2,1,0:T(2,128)(2,1)} %broadcast_in_dim.2), calls=%async_computation.4 | async-start | bytes 65536 | tf_op jit(solution)/shard_map/all_to_all | solution.py:326
  121.4 7.9 %all-to-all-done.4 = bf16[64,2,128]{2,1,0:T(2,128)(2,1)S(1)} async-done(((bf16[64,2,128]{2,1,0:T(2,128)(2,1)}), bf16[64,2,128]{2,1,0:T(2,128)(2,1)S(1)}, u32[]{:S(2)}, u32[]{:S(2)}) %all-to-all-start.4) | async-done | bytes 32800 | tf_op jit(solution)/shard_map/all_to_all | solution.py:326
  129.2 2.9 %shard_map.97 = (bf16[32,2,2176]{2,1,0:T(2,128)(2,1)S(1)}, bf16[32,2,2176]{2,1,0:T(2,128)(2,1)S(1)}) custom-call(s32[1]{0:T(128)} %bitcast.core_ref, bf16[128,128]{1,0:T(8,128)(2,1)S(1)} %bitcast.11, bf16[448,128]{1,0:T(8,128)(2,1)S(1)} %get-tuple-element.25.down_ref, f32[128,896]{1,0:T(8,128)S(1)} %get-tuple-element.26.gate_up_ref, ...), custom_call_target="tpu_custom_call" | custom-call | flops 469762048 | bytes 5242880 | tf_op jit(solution)/shard_map/pallas_call | solution.py:314
  132.9 1.2 collective-permute-done.3
  134.1 1.0 add_convert_fusion
  135.1 3.9 %all-to-all-start.5 = ((bf16[32,2,2176]{2,1,0:T(2,128)(2,1)}), bf16[32,2,2176]{2,1,0:T(2,128)(2,1)S(1)}, u32[]{:S(2)}, u32[]{:S(2)}) async-start(bf16[32,2,2176]{2,1,0:T(2,128)(2,1)} %add_convert_fusion), calls=%async_computation.5 | async-start | bytes 557056 | tf_op jit(solution)/shard_map/all_to_all | solution.py:434
  139.2 8.0 %all-to-all-done.5 = bf16[32,2,2176]{2,1,0:T(2,128)(2,1)S(1)} async-done(((bf16[32,2,2176]{2,1,0:T(2,128)(2,1)}), bf16[32,2,2176]{2,1,0:T(2,128)(2,1)S(1)}, u32[]{:S(2)}, u32[]{:S(2)}) %all-to-all-start.5) | async-done | bytes 278560 | tf_op jit(solution)/shard_map/all_to_all | solution.py:434
  (38 shorter events, 5.1 us)
Async XLA Ops:
  0.0 0.7 copy-start.6
  0.7 0.7 copy-start.8
  1.3 25.8 %copy-start.7 = (s32[128]{0:T(128)S(1)}, s32[128]{0:T(128)}, u32[]{:S(2)}) copy-start(s32[128]{0:T(128)} %attr_ref.1) | copy-start | bytes 1540
  30.5 22.4 %copy-start.9 = (s32[2]{0:T(128)S(1)}, s32[2]{0:T(128)}, u32[]{:S(2)}) copy-start(s32[2]{0:T(128)} %ids.1) | copy-start | bytes 28
  53.5 0.8 copy-start.4
  54.3 17.5 %copy-start = (bf16[2048,448]{0,1:T(8,128)(2,1)S(1)}, bf16[2048,448]{0,1:T(8,128)(2,1)}, u32[]{:S(2)}) copy-start(bf16[2048,448]{0,1:T(8,128)(2,1)} %param.15) | copy-start | bytes 5505028
  54.3 17.5 %all-to-all-start.2 = ((bf16[64,2,2048]{2,1,0:T(2,128)(2,1)}), bf16[64,2,2048]{2,1,0:T(2,128)(2,1)S(1)}, u32[]{:S(2)}, u32[]{:S(2)}) async-start(bf16[64,2,2048]{2,1,0:T(2,128)(2,1)} %copy-done.4), calls=%async_computation.2 | async-start | bytes 1048576 | tf_op jit(solution)/shard_map/all_to_all | solution.py:326
  59.1 1.5 %copy-start.1 = (bf16[448,2048]{1,0:T(8,128)(2,1)S(1)}, bf16[448,2048]{1,0:T(8,128)(2,1)}, u32[]{:S(2)}) copy-start(bf16[448,2048]{1,0:T(8,128)(2,1)} %weight_ref.1) | copy-start | bytes 5505028
  60.6 11.2 %copy-start.5 = (f32[2048]{0:T(1024)S(1)}, f32[2048]{0:T(1024)}, u32[]{:S(2)}) copy-start(f32[2048]{0:T(1024)} %param.14) | copy-start | bytes 24580
  61.5 0.8 copy-start.2
  62.3 35.2 %collective-permute-start = (bf16[448,128]{1,0:T(8,128)(2,1)S(1)}, bf16[448,128]{1,0:T(8,128)(2,1)S(1)}, u32[]{:S(2)}, u32[]{:S(2)}) collective-permute-start(bf16[448,128]{1,0:T(8,128)(2,1)S(1)} %get-tuple-element.22.rest_0_), channel_id=1, source_target_pairs={{0,1},{1,2},{2,3},{3,0},{4,5},{5,6},{6,7},{7,4},{8,9},{9,10},{10,1... | collective-permute-start | bytes 344072 | tf_op jit(solution)/shard_map/ppermute | solution.py:380
  65.3 32.2 %collective-permute-start.1 = (bf16[448,128]{1,0:T(8,128)(2,1)S(1)}, bf16[448,128]{1,0:T(8,128)(2,1)S(1)}, u32[]{:S(2)}, u32[]{:S(2)}) collective-permute-start(bf16[448,128]{1,0:T(8,128)(2,1)S(1)} %get-tuple-element.22.rest_0_), channel_id=1, source_target_pairs={{0,2},{1,3},{2,0},{3,1},{4,6},{5,7},{6,4},{7,5},{8,10},{9,11},{10,... | collective-permute-start | bytes 344072 | tf_op jit(solution)/shard_map/ppermute | solution.py:380
  69.5 28.0 %collective-permute-start.2 = (bf16[448,128]{1,0:T(8,128)(2,1)S(1)}, bf16[448,128]{1,0:T(8,128)(2,1)S(1)}, u32[]{:S(2)}, u32[]{:S(2)}) collective-permute-start(bf16[448,128]{1,0:T(8,128)(2,1)S(1)} %get-tuple-element.22.rest_0_), channel_id=1, source_target_pairs={{0,3},{1,0},{2,1},{3,2},{4,7},{5,4},{6,5},{7,6},{8,11},{9,8},{10,9... | collective-permute-start | bytes 344072 | tf_op jit(solution)/shard_map/ppermute | solution.py:380
  74.1 33.7 %copy-start.11 = (s32[2]{0:T(128)S(1)}, s32[2]{0:T(128)}, u32[]{:S(2)}) copy-start(s32[2]{0:T(128)} %param.12) | copy-start | bytes 28
  74.1 42.1 %copy-start.10 = (s32[2]{0:T(128)S(1)}, s32[2]{0:T(128)}, u32[]{:S(2)}) copy-start(s32[2]{0:T(128)} %param.11) | copy-start | bytes 28
  98.5 17.3 %all-to-all-start.3 = ((f32[64,2,128]{2,1,0:T(2,128)}), f32[64,2,128]{2,1,0:T(2,128)S(1)}, u32[]{:S(2)}, u32[]{:S(2)}) async-start(f32[64,2,128]{2,1,0:T(2,128)} %bitcast.5), calls=%async_computation.3 | async-start | bytes 131072 | tf_op jit(solution)/shard_map/all_to_all | solution.py:326
  117.0 12.3 %all-to-all-start.4 = ((bf16[64,2,128]{2,1,0:T(2,128)(2,1)}), bf16[64,2,128]{2,1,0:T(2,128)(2,1)S(1)}, u32[]{:S(2)}, u32[]{:S(2)}) async-start(bf16[64,2,128]{2,1,0:T(2,128)(2,1)} %broadcast_in_dim.2), calls=%async_computation.4 | async-start | bytes 65536 | tf_op jit(solution)/shard_map/all_to_all | solution.py:326
  129.2 9.7 %copy-start.3 = (bf16[128,2048]{1,0:T(8,128)(2,1)S(1)}, bf16[128,2048]{1,0:T(8,128)(2,1)}, u32[]{:S(2)}) copy-start(bf16[128,2048]{1,0:T(8,128)(2,1)} %copy-done.2) | copy-start | bytes 1572868
  132.1 1.9 %collective-permute-start.3 = (bf16[32,2,2176]{2,1,0:T(2,128)(2,1)S(1)}, bf16[32,2,2176]{2,1,0:T(2,128)(2,1)S(1)}, u32[]{:S(2)}, u32[]{:S(2)}) collective-permute-start(bf16[32,2,2176]{2,1,0:T(2,128)(2,1)S(1)} %get-tuple-element.28), channel_id=1, source_target_pairs={{0,4},{4,0},{8,12},{12,8},{16,20},{20,16},{24,28},{28,24},{32,36},... | collective-permute-start | bytes 835592 | tf_op jit(solution)/shard_map/ppermute | solution.py:431
  135.1 12.1 %all-to-all-start.5 = ((bf16[32,2,2176]{2,1,0:T(2,128)(2,1)}), bf16[32,2,2176]{2,1,0:T(2,128)(2,1)S(1)}, u32[]{:S(2)}, u32[]{:S(2)}) async-start(bf16[32,2,2176]{2,1,0:T(2,128)(2,1)} %add_convert_fusion), calls=%async_computation.5 | async-start | bytes 557056 | tf_op jit(solution)/shard_map/all_to_all | solution.py:434
